TPU v7x, 512 devices: a whole 4x8x8 slice. The times are simulated.
512 devices in a mesh: space: 16 (over y, z_hi), mom: 32 (over z_lo, x, core).
Axes of the slice: x: 4, y: 8, z: 8 (z_hi: 2, z_lo: 4; z = z_hi * 4 + z_lo), core: 2. Of those that a mesh axis runs over, the one named last changes fastest.
Arguments:
- density: float32 [256, 256, 2048], P('mom', None, 'space'), may hold values from -6 to 6
- mode_waves: int32 [16, 2], replicated, may hold values from -7 to 7
- mode_amplitudes: float32 [16], replicated, may hold values from -3 to 3
- mode_phases: float32 [16], replicated, may hold values from -3.140625 to 3.140625
Outputs:
- time_rate: float32 [256, 256, 2048], P('mom', None, 'space')
All inputs are finite; a program needn't handle non-finite values.
Results may differ from a plain program's by a relative error of at most 0.0003.
Values sent between devices are 32-bit elements; how exact they have to be, the bound alone decides.
No kernel may reach another device: no remote copies, remote signals or barrier semaphores. Data moves between devices by JAX's collectives and lax.ppermute only.
A program may use at most 64 MiB of HBM per device.

v0:
```python
import math

import jax
import jax.numpy as jnp
import ml_dtypes
import numpy as np
from jax import lax
from jax.experimental import pallas as pl
from jax.experimental.pallas import tpu as pltpu
from jax.sharding import PartitionSpec as P

NY = 16
POINTS = 256
HALF = POINTS // 2
DAMPING = 0.5
FRICTION = 0.5
MINUS = ((-3, -2.0), (-2, 15.0), (-1, -60.0), (0, 20.0), (1, 30.0), (2, -3.0))
PLUS = ((3, 2.0), (2, -15.0), (1, 60.0), (0, -20.0), (-1, -30.0), (-2, 3.0))
F32 = jnp.float32
BF16 = jnp.bfloat16
HIGHEST_PRECISION = lax.Precision.HIGHEST


def wide(table):
    high = table.astype(ml_dtypes.bfloat16)
    low = (table - high.astype(np.float64)).astype(ml_dtypes.bfloat16)
    return np.concatenate([high, high, low], axis=1)


def real_fourier():
    k = np.arange(POINTS)
    m = np.arange(HALF)
    angles = 2.0 * np.pi / POINTS * (m[:, None] * k[None, :] % POINTS)
    cosine, sine = np.cos(angles), -np.sin(angles)
    sine[0] = 1.0 - 2.0 * (k % 2)
    forward = np.concatenate([cosine, sine], axis=0)
    weight = np.full((HALF,), 2.0)
    weight[0] = 1.0
    inverse = (forward * np.concatenate([weight, weight])[:, None] / POINTS).T
    return forward, inverse


def interleaved(rows):
    return np.stack([rows[:HALF], rows[HALF:]], axis=1).reshape(POINTS, -1)


def friction_matrix():
    speed = (2.0 * np.arange(POINTS) - POINTS + 1) / POINTS
    result = np.zeros((POINTS, POINTS))
    k = np.arange(POINTS - 1)
    result[k, k + 1] = FRICTION * speed[k + 1]
    result[k + 1, k] = -FRICTION * speed[k]
    return result


def row_matrix(stencil, first_row, rows, out_rows):
    result = np.zeros((rows * NY, out_rows * NY))
    for out_row in range(out_rows):
        for offset, weight in stencil:
            row = out_row + offset - first_row
            if 0 <= row < rows:
                for column in range(NY):
                    result[row * NY + column, out_row * NY + column] = weight
    return result


def column_matrix(stencil, rows):
    result = np.zeros((rows * NY, rows * NY))
    for row in range(rows):
        for column in range(NY):
            for offset, weight in stencil:
                result[row * NY + (column + offset) % NY, row * NY + column] += weight
    return result


def bf16_table(table):
    return jnp.asarray(table.astype(ml_dtypes.bfloat16))


def tables(rows_dev):
    forward, inverse = real_fourier()
    result = {}
    result["forward_second"] = jnp.asarray(wide(interleaved(forward)))
    result["inverse_second"] = jnp.asarray(wide(interleaved(inverse.T).T))
    result["forward_first"] = jnp.asarray(wide(forward))
    friction = friction_matrix().astype(ml_dtypes.bfloat16)
    result["inverse_first"] = jnp.asarray(
        np.concatenate([wide(inverse), friction, friction], axis=1)
    )
    result["friction"] = jnp.asarray(np.concatenate([friction, friction], axis=1))
    rows = 2 * rows_dev
    edge = rows_dev // 2
    inner, halo = [], []
    for stencil in (PLUS, MINUS):
        inner.append(row_matrix(stencil, 0, rows, rows))
        before = row_matrix(stencil, -edge, edge, rows)
        after = row_matrix(stencil, rows, edge, rows)
        none = np.zeros_like(before)
        even = np.concatenate([before, none, after, none], axis=0)
        odd = np.concatenate([none, before, none, after], axis=0)
        halo.append(np.stack([even, odd]))
    result["row_inner"] = bf16_table(np.stack(inner))
    result["row_halo"] = bf16_table(np.stack(halo))
    result["column_shift"] = bf16_table(
        np.stack(
            [
                np.concatenate([column_matrix(s, rows_dev)] * 2, axis=0)
                for s in (PLUS, MINUS)
            ]
        )
    )
    return result


def split(value):
    high = value.astype(BF16)
    low = (value - high.astype(F32)).astype(BF16)
    return high, low


def dot(left, right):
    return jnp.dot(left, right, preferred_element_type=F32)


def speed_over_60(first, count, width):
    index = first + lax.broadcasted_iota(jnp.int32, (count, width), 0)
    return (2 * index - (POINTS - 1)).astype(F32) * (1.0 / (60 * POINTS))


def forward_kernel(u_ref, table_ref, out_ref, x_ref):
    planes, _, cells = u_ref.shape
    for k in range(planes):
        high, low = split(u_ref[k])
        x_ref[0:POINTS, k * cells : (k + 1) * cells] = high
        x_ref[POINTS : 2 * POINTS, k * cells : (k + 1) * cells] = low
    result = dot(table_ref[:, : 2 * POINTS], x_ref[...]) + dot(
        table_ref[:, 2 * POINTS :], x_ref[0:POINTS, :]
    )
    for k in range(planes):
        out_ref[pl.ds(k, POINTS, stride=planes), :] = result[:, k * cells : (k + 1) * cells]


def backward_kernel(w_ref, local_ref, table_ref, out_ref, x_ref):
    planes, _, cells = local_ref.shape
    for k in range(planes):
        high, low = split(w_ref[pl.ds(k, POINTS, stride=planes), :])
        x_ref[0:POINTS, k * cells : (k + 1) * cells] = high
        x_ref[POINTS : 2 * POINTS, k * cells : (k + 1) * cells] = low
    result = dot(table_ref[:, : 2 * POINTS], x_ref[...]) + dot(
        table_ref[:, 2 * POINTS :], x_ref[0:POINTS, :]
    )
    for k in range(planes):
        out_ref[k] = result[:, k * cells : (k + 1) * cells] + local_ref[k]


def local_kernel(u_ref, friction_ref, shift_ref, out_ref):
    planes, _, cells = u_ref.shape
    for k in range(planes):
        high, low = split(u_ref[k])
        friction = dot(friction_ref[...], jnp.concatenate([high, low], axis=0))
        both = jnp.concatenate([high, low], axis=1)
        for side in range(2):
            part = slice(side * HALF, (side + 1) * HALF)
            moved = dot(both[part], shift_ref[side])
            out_ref[k, part, :] = friction[part] - moved * speed_over_60(
                side * HALF, HALF, cells
            )


def halo_kernel(r_ref, up_ref, down_ref):
    owners = r_ref.shape[0] // 2
    cells = r_ref.shape[3]
    lower = lax.broadcasted_iota(jnp.int32, (POINTS, cells), 1) < cells // 2
    for pair in range(2):
        first, second = (
            r_ref[owners:, 2 * pair + part].reshape(POINTS, cells) for part in range(2)
        )
        up_ref[pair] = jnp.where(lower, pltpu.roll(first, cells // 2, 1), second)
        first, second = (
            r_ref[:owners, 2 * pair + part].reshape(POINTS, cells) for part in range(2)
        )
        down_ref[pair] = jnp.where(lower, first, pltpu.roll(second, cells // 2, 1))


def load_columns(r_ref, x_ref):
    owners = r_ref.shape[0] // 2
    cells = r_ref.shape[3]
    for q in range(4):
        for side in range(2):
            value = r_ref[side * owners : (side + 1) * owners, q].reshape(POINTS, cells)
            high, low = split(value)
            at = (2 * q + side) * cells
            x_ref[0:POINTS, at : at + cells] = high
            x_ref[POINTS : 2 * POINTS, at : at + cells] = low


def spectral_kernel(damp_ref, r_ref, table_ref, symbol_ref, x_ref, y_ref):
    load_columns(r_ref, x_ref)
    spectrum = dot(table_ref[:, : 2 * POINTS], x_ref[...]) + dot(
        table_ref[:, 2 * POINTS :], x_ref[0:POINTS, :]
    )
    width = spectrum.shape[1] // 4
    row = lax.broadcasted_iota(jnp.int32, (HALF, width), 0)
    scale = DAMPING / (HALF * HALF)
    damp_real = scale * (row * row).astype(F32)
    row_imag = jnp.where(row == 0, HALF, row)
    damp_imag = scale * (row_imag * row_imag).astype(F32)
    for slot in range(2):
        qa, qb = 2 * slot, 2 * slot + 1
        real_a, imag_a = (
            spectrum[h * HALF : (h + 1) * HALF, qa * width : (qa + 1) * width]
            for h in range(2)
        )
        real_b, imag_b = (
            spectrum[h * HALF : (h + 1) * HALF, qb * width : (qb + 1) * width]
            for h in range(2)
        )
        odd_a, odd_b = symbol_ref[slot, 0], symbol_ref[slot, 1]
        even_real, even_imag = symbol_ref[slot, 2], symbol_ref[slot, 3]
        da, db = damp_ref[qa], damp_ref[qb]
        results = (
            (qa, 0, -odd_a * imag_a - even_real * real_b - (damp_real + da) * real_a),
            (qa, 1, odd_a * real_a - even_imag * imag_b - (damp_imag + da) * imag_a),
            (qb, 0, -odd_b * imag_b + even_real * real_a - (damp_real + db) * real_b),
            (qb, 1, odd_b * real_b + even_imag * imag_a - (damp_imag + db) * imag_b),
        )
        for q, half, value in results:
            high, low = split(value)
            at = q * width
            y_ref[half * HALF : (half + 1) * HALF, at : at + width] = high
            y_ref[POINTS + half * HALF : POINTS + (half + 1) * HALF, at : at + width] = low


def combine_kernel(x_ref, y_ref, before_ref, after_ref, table_ref, inner_ref, halo_ref, out_ref):
    width = x_ref.shape[1] // 4
    cells = width // 2
    owners = out_ref.shape[0] // 2
    result = (
        dot(table_ref[:, : 2 * POINTS], y_ref[...])
        + dot(table_ref[:, 2 * POINTS : 3 * POINTS], y_ref[0:POINTS, :])
        + dot(table_ref[:, 3 * POINTS :], x_ref[...])
    )
    halos = []
    for pair in range(2):
        before_high, before_low = split(before_ref[pair])
        after_high, after_low = split(after_ref[pair])
        halos.append(
            (
                jnp.concatenate([before_high, after_high], axis=1),
                jnp.concatenate([before_low, after_low], axis=1),
            )
        )
    for q in range(4):
        columns = slice(q * width, (q + 1) * width)
        for side in range(2):
            part = slice(side * HALF, (side + 1) * HALF)
            low = slice(POINTS + side * HALF, POINTS + (side + 1) * HALF)
            inner, halo = inner_ref[side], halo_ref[side, q % 2]
            high_halo, low_halo = halos[q // 2]
            moved = (
                dot(x_ref[part, columns], inner)
                + dot(x_ref[low, columns], inner)
                + dot(high_halo[part], halo)
                + dot(low_halo[part], halo)
            )
            value = result[part, columns] - moved * speed_over_60(side * HALF, HALF, width)
            rows = owners // 2
            for band in range(2):
                out_ref[
                    band * owners + side * rows : band * owners + (side + 1) * rows, q
                ] = value[:, band * cells : (band + 1) * cells].reshape(rows, -1, cells)


VMEM_SPEC = pl.BlockSpec(memory_space=pltpu.VMEM)
SMEM_SPEC = pl.BlockSpec(memory_space=pltpu.SMEM)


def call(kernel, shapes, inputs, scratch=(), flops=1, smem=0, name=None):
    bytes_accessed = sum(v.size * v.dtype.itemsize for v in inputs)
    shapes = [jax.ShapeDtypeStruct(*s) for s in shapes]
    single = len(shapes) == 1
    return pl.pallas_call(
        kernel,
        out_shape=shapes[0] if single else shapes,
        in_specs=[SMEM_SPEC] * smem + [VMEM_SPEC] * (len(inputs) - smem),
        out_specs=VMEM_SPEC if single else [VMEM_SPEC] * len(shapes),
        scratch_shapes=list(scratch),
        cost_estimate=pl.CostEstimate(
            flops=flops, bytes_accessed=2 * bytes_accessed, transcendentals=0
        ),
        name=name,
    )(*inputs)


def symbol_table(mode_waves, mode_amplitudes, mode_phases, first_slot, first_row, rows, total_rows):
    local = jnp.arange(rows * NY, dtype=jnp.int32)
    row, column = first_row + local // NY, local % NY
    turn_rows = mode_waves[:, 0:1] * row[None, :] % total_rows
    turn_columns = mode_waves[:, 1:2] * column[None, :] % NY
    angles = (
        2.0
        * math.pi
        * (turn_rows.astype(F32) / total_rows + turn_columns.astype(F32) / NY)
        + mode_phases[:, None]
    )
    cell_factor = mode_amplitudes[:, None] * jnp.sin(angles)
    scale = math.pi / POINTS

    def turned(waves, frequency):
        return scale * (waves * frequency % (2 * POINTS)).astype(F32)

    first_waves, second_waves = mode_waves[None, :, 0], mode_waves[None, :, 1]
    real_freq = jnp.arange(HALF, dtype=jnp.int32)[:, None]
    imag_freq = jnp.where(real_freq == 0, HALF, real_freq)
    odd_first = jnp.sin(turned(first_waves, real_freq))
    even_real = jnp.cos(turned(first_waves, real_freq))
    even_imag = jnp.cos(turned(first_waves, imag_freq))
    slots = first_slot + jnp.arange(2, dtype=jnp.int32)[:, None]
    slots_b = jnp.where(slots == 0, HALF, slots)
    odd_second = jnp.sin(turned(second_waves, slots))
    even_a = jnp.cos(turned(second_waves, slots))
    even_b = jnp.cos(turned(second_waves, slots_b))
    factors = jnp.stack(
        [
            odd_first[None] * even_a[:, None],
            odd_first[None] * even_b[:, None],
            even_real[None] * odd_second[:, None],
            even_imag[None] * odd_second[:, None],
        ],
        axis=1,
    )
    symbol = jnp.dot(
        factors.reshape(8 * HALF, -1), cell_factor, precision=HIGHEST_PRECISION
    ).reshape(2, 4, HALF, rows * NY)
    damp = DAMPING / (HALF * HALF) * jnp.stack(
        [slots * slots, slots_b * slots_b], axis=1
    ).reshape(4).astype(F32)
    return symbol, damp


def stage_forward(density, table):
    planes, points, cells = density.shape
    width = planes * cells
    sent = call(
        forward_kernel,
        [((points * planes, cells), F32)],
        (density, table["forward_second"]),
        (pltpu.VMEM((2 * points, width), BF16),),
        6 * points * points * width,
        name="forward_second",
    )
    return sent.reshape(points // 4, 4, planes, cells)


def stage_local(density, table):
    planes, points, cells = density.shape
    return call(
        local_kernel,
        [((planes, points, cells), F32)],
        (density, table["friction"], table["column_shift"]),
        flops=6 * points * points * planes * cells,
        name="local_part",
    )


def stage_halo(columns):
    cells = columns.shape[3]
    return call(
        halo_kernel, [((2, POINTS, cells), F32)] * 2, (columns,), name="halo_pack"
    )


def stage_spectral(damp, columns, symbol, table):
    width = 8 * columns.shape[3]
    return call(
        spectral_kernel,
        [((2 * POINTS, width), BF16)] * 2,
        (damp, columns, table["forward_first"], symbol),
        flops=6 * POINTS * POINTS * width,
        smem=1,
        name="spectral",
    )


def stage_combine(x, y, before, after, table, planes, members):
    width = x.shape[1]
    return call(
        combine_kernel,
        [((members, 4, planes, width // 8), F32)],
        (x, y, before, after, table["inverse_first"], table["row_inner"], table["row_halo"]),
        flops=18 * POINTS * POINTS * width,
        name="combine",
    )


def stage_backward(panels, here, table):
    planes, points, cells = here.shape
    width = planes * cells
    return call(
        backward_kernel,
        [((planes, points, cells), F32)],
        (panels.reshape(points * planes, cells), here, table["inverse_second"]),
        (pltpu.VMEM((2 * points, width), BF16),),
        6 * points * points * width,
        name="inverse_second",
    )


def local(density, mode_waves, mode_amplitudes, mode_phases):
    planes, _, cells = density.shape
    rows_dev = cells // NY
    group = ("pair", "mom")
    members = lax.axis_size(group)
    strips = lax.axis_size("y")
    table = tables(rows_dev)

    sent = stage_forward(density, table)
    columns = lax.all_to_all(sent, group, split_axis=0, concat_axis=0, tiled=True)
    here = stage_local(density, table)
    position = lax.axis_index("pair") * lax.axis_size("mom") + lax.axis_index("mom")
    symbol, damp = symbol_table(
        mode_waves,
        mode_amplitudes,
        mode_phases,
        2 * position,
        lax.axis_index("y") * (2 * rows_dev),
        2 * rows_dev,
        2 * rows_dev * strips,
    )
    up, down = stage_halo(columns)
    before = lax.ppermute(up, "y", [(i, (i + 1) % strips) for i in range(strips)])
    after = lax.ppermute(down, "y", [((i + 1) % strips, i) for i in range(strips)])
    x, y = stage_spectral(damp, columns, symbol, table)
    back = stage_combine(x, y, before, after, table, planes, members)
    panels = lax.all_to_all(back, group, split_axis=0, concat_axis=0, tiled=True)
    return stage_backward(panels, here, table)


def solution(mesh):
    bands = mesh.shape["space"]
    finer = jax.sharding.Mesh(
        mesh.devices.reshape(bands // 2, 2, mesh.shape["mom"]), ("y", "pair", "mom")
    )
    return jax.shard_map(
        local,
        mesh=finer,
        in_specs=(P("mom", None, ("y", "pair")), P(), P(), P()),
        out_specs=P("mom", None, ("y", "pair")),
        check_vma=False,
    )
```

profile of v0, /device:TPU:24, one launch (start us, length us, event | category | flops | bytes accessed | tf_op | source)
XLA Modules:
  0.0 108.4 jit_solution(17865334464517430003)
XLA Ops:
  0.0 2.9 %forward_second.1 = f32[2048,128]{1,0:T(8,128)} custom-call(f32[8,256,128]{2,1,0:T(8,128)} %u_ref.3, bf16[256,768]{1,0:T(8,128)(2,1)} %constant.138.clone.table_ref), custom_call_target="tpu_custom_call" | custom-call | flops 402653184 | bytes 2883584 | tf_op jit(solution)/shard_map/forward_second/pallas_call | solution.py:282
  2.9 13.8 %all-to-all-start = ((f32[64,4,8,128]{3,2,1,0:T(8,128)}), f32[64,4,8,128]{3,2,1,0:T(8,128)S(1)}, u32[]{:S(2)}, u32[]{:S(2)}) async-start(f32[64,4,8,128]{3,2,1,0:T(8,128)} %bitcast.14), calls=%async_computation | async-start | bytes 2097152 | tf_op jit(solution)/shard_map/all_to_all | solution.py:418
  16.7 0.1 fusion.65
  16.8 0.6 mul.279.damp_ref
  17.5 0.7 copy-done.4
  18.2 0.1 fusion.68
  18.3 0.1 fusion.53
  18.4 0.1 broadcast_multiply_fusion.3
  18.6 27.0 %all-to-all-done.r_ref = f32[64,4,8,128]{3,2,1,0:T(8,128)S(1)} async-done(((f32[64,4,8,128]{3,2,1,0:T(8,128)}), f32[64,4,8,128]{3,2,1,0:T(8,128)S(1)}, u32[]{:S(2)}, u32[]{:S(2)}) %all-to-all-start) | async-done | bytes 1048608 | tf_op jit(solution)/shard_map/all_to_all | solution.py:418
  45.6 1.0 copy-done
  46.6 2.2 %halo_pack.1 = (f32[2,256,128]{2,1,0:T(8,128)}, f32[2,256,128]{2,1,0:T(8,128)}) custom-call(f32[64,4,8,128]{3,2,1,0:T(8,128)} %copy-done), custom_call_target="tpu_custom_call" | custom-call | flops 1 | bytes 2097152 | tf_op jit(solution)/shard_map/halo_pack/pallas_call | solution.py:282
  48.7 4.7 %collective-permute-start = (f32[2,256,128]{2,1,0:T(8,128)}, f32[2,256,128]{2,1,0:T(8,128)S(1)}, u32[]{:S(2)}, u32[]{:S(2)}) collective-permute-start(f32[2,256,128]{2,1,0:T(8,128)} %get-tuple-element.11), channel_id=1, source_target_pairs={{0,64},{64,128},{128,192},{192,256},{256,320},{320,384},{384,448},... | collective-permute-start | bytes 786440 | tf_op jit(solution)/shard_map/ppermute | solution.py:431
  53.4 1.9 %collective-permute-start.1 = (f32[2,256,128]{2,1,0:T(8,128)}, f32[2,256,128]{2,1,0:T(8,128)S(1)}, u32[]{:S(2)}, u32[]{:S(2)}) collective-permute-start(f32[2,256,128]{2,1,0:T(8,128)} %get-tuple-element.12), channel_id=1, source_target_pairs={{64,0},{128,64},{192,128},{256,192},{320,256},{384,320},{448,384},... | collective-permute-start | bytes 786440 | tf_op jit(solution)/shard_map/ppermute | solution.py:432
  55.4 0.6 copy-done.5
  56.0 2.1 %fusion.symbol_ref = f32[2,4,128,256]{3,2,1,0:T(8,128)} fusion(f32[2,1,128,16]{2,3,1,0:T(8,128)S(1)} %get-tuple-element.18, f32[2,1,128,16]{2,3,1,0:T(8,128)S(1)} %get-tuple-element.17, f32[2,1,128,16]{2,3,1,0:T(8,128)S(1)} %get-tuple-element.14, f32[2,1,128,16]{2,3,1,0:T(8,128)S(1)} %get-tuple-element.13, f32[16]{0:T(128)S(1)} %copy-done.5, ...), kind=kOutput, calls=%fused_computation | convolution fusion | flops 50511872 | bytes 1116416 | tf_op jit(solution)/shard_map/dot_general | solution.py:332
  58.1 3.5 %spectral.1 = (bf16[512,1024]{1,0:T(8,128)(2,1)}, bf16[512,1024]{1,0:T(8,128)(2,1)}) custom-call(f32[4]{0:T(128)} %mul.279.damp_ref, f32[64,4,8,128]{3,2,1,0:T(8,128)} %copy-done, bf16[256,768]{1,0:T(8,128)(2,1)} %constant.140.clone.table_ref, f32[2,4,128,256]{3,2,1,0:T(8,128)} %fusion.symbol_ref), custom_call_target="tpu_custom_call" | custom-call | flops 402653184 | bytes 4980768 | tf_op jit(solution)/shard_map/spectral/pallas_call | solution.py:282
  61.6 2.4 %collective-permute-done.1.after_ref = f32[2,256,128]{2,1,0:T(8,128)S(1)} collective-permute-done((f32[2,256,128]{2,1,0:T(8,128)}, f32[2,256,128]{2,1,0:T(8,128)S(1)}, u32[]{:S(2)}, u32[]{:S(2)}) %collective-permute-start.1) | collective-permute-done | bytes 262176 | tf_op jit(solution)/shard_map/ppermute | solution.py:432
  64.0 0.7 copy-done.3
  64.7 4.5 %combine.1 = f32[64,4,8,128]{3,2,1,0:T(8,128)} custom-call(bf16[512,1024]{1,0:T(8,128)(2,1)} %get-tuple-element.9.x_ref, bf16[512,1024]{1,0:T(8,128)(2,1)} %get-tuple-element.10.y_ref, f32[2,256,128]{2,1,0:T(8,128)} %copy-done.2, f32[2,256,128]{2,1,0:T(8,128)} %copy-done.3, bf16[256,1280]{1,0:T(8,128)(2,1)} %constant.141.clone.table_ref, ...), custom_call_target="tpu_custom_call" | custom-call | flops 1207959552 | bytes 8126464 | tf_op jit(solution)/shard_map/combine/pallas_call | solution.py:282
  69.3 5.8 %all-to-all-start.1 = ((f32[64,4,8,128]{3,2,1,0:T(8,128)}), f32[64,4,8,128]{3,2,1,0:T(8,128)S(1)}, u32[]{:S(2)}, u32[]{:S(2)}) async-start(f32[64,4,8,128]{3,2,1,0:T(8,128)} %combine.1), calls=%async_computation.1 | async-start | bytes 2097152 | tf_op jit(solution)/shard_map/all_to_all | solution.py:435
  75.1 3.3 %local_part.1.local_ref = f32[8,256,128]{2,1,0:T(8,128)} custom-call(f32[8,256,128]{2,1,0:T(8,128)} %u_ref.3, bf16[256,512]{1,0:T(8,128)(2,1)} %constant.142.clone.friction_ref, bf16[2,256,128]{2,1,0:T(8,128)(2,1)} %constant.145.clone.shift_ref), custom_call_target="tpu_custom_call" | custom-call | flops 402653184 | bytes 2883584 | tf_op jit(solution)/shard_map/local_part/pallas_call | solution.py:282
  78.4 25.6 %all-to-all-done.1 = f32[64,4,8,128]{3,2,1,0:T(8,128)S(1)} async-done(((f32[64,4,8,128]{3,2,1,0:T(8,128)}), f32[64,4,8,128]{3,2,1,0:T(8,128)S(1)}, u32[]{:S(2)}, u32[]{:S(2)}) %all-to-all-start.1) | async-done | bytes 1048608 | tf_op jit(solution)/shard_map/all_to_all | solution.py:435
  104.0 1.0 copy-done.1
  105.0 3.4 %inverse_second.1 = f32[8,256,128]{2,1,0:T(8,128)} custom-call(f32[2048,128]{1,0:T(8,128)} %bitcast.13, f32[8,256,128]{2,1,0:T(8,128)} %local_part.1.local_ref, bf16[256,768]{1,0:T(8,128)(2,1)} %constant.139.clone.table_ref), custom_call_target="tpu_custom_call" | custom-call | flops 402653184 | bytes 4980736 | tf_op jit(solution)/shard_map/inverse_second/pallas_call | solution.py:282
  (16 shorter events, 0.1 us)
Async XLA Ops:
  2.9 42.7 %all-to-all-start = ((f32[64,4,8,128]{3,2,1,0:T(8,128)}), f32[64,4,8,128]{3,2,1,0:T(8,128)S(1)}, u32[]{:S(2)}, u32[]{:S(2)}) async-start(f32[64,4,8,128]{3,2,1,0:T(8,128)} %bitcast.14), calls=%async_computation | async-start | bytes 2097152 | tf_op jit(solution)/shard_map/all_to_all | solution.py:418
  17.5 0.7 copy-start.4
  45.6 1.0 copy-start
  48.7 12.9 %collective-permute-start = (f32[2,256,128]{2,1,0:T(8,128)}, f32[2,256,128]{2,1,0:T(8,128)S(1)}, u32[]{:S(2)}, u32[]{:S(2)}) collective-permute-start(f32[2,256,128]{2,1,0:T(8,128)} %get-tuple-element.11), channel_id=1, source_target_pairs={{0,64},{64,128},{128,192},{192,256},{256,320},{320,384},{384,448},... | collective-permute-start | bytes 786440 | tf_op jit(solution)/shard_map/ppermute | solution.py:431
  53.4 10.6 %collective-permute-start.1 = (f32[2,256,128]{2,1,0:T(8,128)}, f32[2,256,128]{2,1,0:T(8,128)S(1)}, u32[]{:S(2)}, u32[]{:S(2)}) collective-permute-start(f32[2,256,128]{2,1,0:T(8,128)} %get-tuple-element.12), channel_id=1, source_target_pairs={{64,0},{128,64},{192,128},{256,192},{320,256},{384,320},{448,384},... | collective-permute-start | bytes 786440 | tf_op jit(solution)/shard_map/ppermute | solution.py:432
  55.4 0.7 copy-start.5
  55.4 0.7 copy-start.6
  61.6 2.4 %copy-start.2 = (f32[2,256,128]{2,1,0:T(8,128)}, f32[2,256,128]{2,1,0:T(8,128)S(1)}, u32[]{:S(2)}) copy-start(f32[2,256,128]{2,1,0:T(8,128)S(1)} %collective-permute-done.before_ref) | copy-start | bytes 786436
  64.0 0.7 copy-start.3
  69.3 34.7 %all-to-all-start.1 = ((f32[64,4,8,128]{3,2,1,0:T(8,128)}), f32[64,4,8,128]{3,2,1,0:T(8,128)S(1)}, u32[]{:S(2)}, u32[]{:S(2)}) async-start(f32[64,4,8,128]{3,2,1,0:T(8,128)} %combine.1), calls=%async_computation.1 | async-start | bytes 2097152 | tf_op jit(solution)/shard_map/all_to_all | solution.py:435
  104.0 1.0 copy-start.1
where the time goes:
time: 109 us; the launch traced here: 108 us
  waiting for transfers between devices  55 us (50%)
  starting transfers between devices  26.2 us (24%)
  Pallas kernels  19.7 us (18%)
  local copies, waits for them, and re-layouts  4.64 us (4%)
  matrix products  2.1 us (2%)
    all_to_all x1, waiting for transfers between devices, local(): lax.all_to_all(sent, group, split_axis=0, concat_axis=0, tiled=True)  27 us
    all_to_all x1, waiting for transfers between devices, local(): lax.all_to_all(back, group, split_axis=0, concat_axis=0, tiled=True)  25.6 us
    pallas_call x6, Pallas kernels, call(): pl.pallas_call(kernel, out_shape=shapes[0] if single else shapes, in_spec...  19.7 us
    all_to_all x1, starting transfers between devices, local(): lax.all_to_all(sent, group, split_axis=0, concat_axis=0, tiled=True)  13.8 us
    all_to_all x1, starting transfers between devices, local(): lax.all_to_all(back, group, split_axis=0, concat_axis=0, tiled=True)  5.84 us
    ppermute x1, starting transfers between devices, local(): lax.ppermute(up, 'y', [(i, (i + 1) % strips) for i in range(strips)])  4.69 us
    unnamed x14, local copies, waits for them, and re-layouts  3.99 us
    ppermute x1, waiting for transfers between devices, local(): lax.ppermute(down, 'y', [((i + 1) % strips, i) for i in range(strips)])  2.44 us
  transfers between devices with their start and end apart: 4, of which 3 were waited for; matrix products, arithmetic and copies ran while one was open for 3% of the time, Pallas kernels for 6%

commit v1 on v0

--- a/solution.py
+++ b/solution.py
@@ -19,6 +19,9 @@
 F32 = jnp.float32
 BF16 = jnp.bfloat16
 HIGHEST_PRECISION = lax.Precision.HIGHEST
+FORWARD_STEPS = 4
+BACKWARD_STEPS = 2
+SENT_ON_CHIP = True
 
 
 def wide(table):
@@ -53,11 +56,11 @@
     return result
 
 
-def row_matrix(stencil, first_row, rows, out_rows):
-    result = np.zeros((rows * NY, out_rows * NY))
-    for out_row in range(out_rows):
+def row_matrix(stencil, rows):
+    result = np.zeros((rows * NY, rows * NY))
+    for out_row in range(rows):
         for offset, weight in stencil:
-            row = out_row + offset - first_row
+            row = out_row + offset
             if 0 <= row < rows:
                 for column in range(NY):
                     result[row * NY + column, out_row * NY + column] = weight
@@ -89,18 +92,9 @@
     )
     result["friction"] = jnp.asarray(np.concatenate([friction, friction], axis=1))
     rows = 2 * rows_dev
-    edge = rows_dev // 2
-    inner, halo = [], []
-    for stencil in (PLUS, MINUS):
-        inner.append(row_matrix(stencil, 0, rows, rows))
-        before = row_matrix(stencil, -edge, edge, rows)
-        after = row_matrix(stencil, rows, edge, rows)
-        none = np.zeros_like(before)
-        even = np.concatenate([before, none, after, none], axis=0)
-        odd = np.concatenate([none, before, none, after], axis=0)
-        halo.append(np.stack([even, odd]))
-    result["row_inner"] = bf16_table(np.stack(inner))
-    result["row_halo"] = bf16_table(np.stack(halo))
+    result["row_inner"] = bf16_table(
+        np.stack([row_matrix(stencil, rows) for stencil in (PLUS, MINUS)])
+    )
     result["column_shift"] = bf16_table(
         np.stack(
             [
@@ -127,30 +121,34 @@
     return (2 * index - (POINTS - 1)).astype(F32) * (1.0 / (60 * POINTS))
 
 
-def forward_kernel(u_ref, table_ref, out_ref, x_ref):
+def forward_kernel(u_ref, table_ref, out_ref):
     planes, _, cells = u_ref.shape
+    first = pl.program_id(0) * planes
+    parts = [split(u_ref[k]) for k in range(planes)]
+    high, low = (jnp.concatenate(values, axis=1) for values in zip(*parts))
+    result = dot(table_ref[:, : 2 * POINTS], jnp.concatenate([high, low], axis=0)) + dot(
+        table_ref[:, 2 * POINTS :], high
+    )
+    stride = out_ref.shape[0] // POINTS
     for k in range(planes):
-        high, low = split(u_ref[k])
-        x_ref[0:POINTS, k * cells : (k + 1) * cells] = high
-        x_ref[POINTS : 2 * POINTS, k * cells : (k + 1) * cells] = low
-    result = dot(table_ref[:, : 2 * POINTS], x_ref[...]) + dot(
-        table_ref[:, 2 * POINTS :], x_ref[0:POINTS, :]
+        out_ref[pl.ds(first + k, POINTS, stride=stride), :] = result[
+            :, k * cells : (k + 1) * cells
+        ]
+
+
+def backward_kernel(w_ref, local_ref, table_ref, out_ref):
+    planes, _, cells = out_ref.shape
+    first = pl.program_id(0) * planes
+    stride = w_ref.shape[0] // POINTS
+    parts = [
+        split(w_ref[pl.ds(first + k, POINTS, stride=stride), :]) for k in range(planes)
+    ]
+    high, low = (jnp.concatenate(values, axis=1) for values in zip(*parts))
+    result = dot(table_ref[:, : 2 * POINTS], jnp.concatenate([high, low], axis=0)) + dot(
+        table_ref[:, 2 * POINTS :], high
     )
     for k in range(planes):
-        out_ref[pl.ds(k, POINTS, stride=planes), :] = result[:, k * cells : (k + 1) * cells]
-
-
-def backward_kernel(w_ref, local_ref, table_ref, out_ref, x_ref):
-    planes, _, cells = local_ref.shape
-    for k in range(planes):
-        high, low = split(w_ref[pl.ds(k, POINTS, stride=planes), :])
-        x_ref[0:POINTS, k * cells : (k + 1) * cells] = high
-        x_ref[POINTS : 2 * POINTS, k * cells : (k + 1) * cells] = low
-    result = dot(table_ref[:, : 2 * POINTS], x_ref[...]) + dot(
-        table_ref[:, 2 * POINTS :], x_ref[0:POINTS, :]
-    )
-    for k in range(planes):
-        out_ref[k] = result[:, k * cells : (k + 1) * cells] + local_ref[k]
+        out_ref[k] = result[:, k * cells : (k + 1) * cells] + local_ref[first + k]
 
 
 def local_kernel(u_ref, friction_ref, shift_ref, out_ref):
@@ -167,19 +165,51 @@
             )
 
 
-def halo_kernel(r_ref, up_ref, down_ref):
+def lane_select(values, lane, width):
+    result = values[0]
+    for index, value in enumerate(values[1:], 1):
+        result = jnp.where(lane >= index * width, value, result)
+    return result
+
+
+def turn(value, shift):
+    shift %= value.shape[1]
+    return pltpu.roll(value, shift, 1) if shift else value
+
+
+def pack(r_ref, near, far, side):
+    cells = r_ref.shape[3]
+    lane = lax.broadcasted_iota(jnp.int32, (POINTS, cells), 1)
+    columns = [r_ref[:, q].reshape(POINTS, cells) for q in range(4)]
+    wide_part = lane_select(
+        [turn(v, 2 * NY * q - near) for q, v in enumerate(columns)], lane, 2 * NY
+    )
+    quarter = HALF // 2
+    lane = lane[:quarter]
+    thin_part = lane_select(
+        [
+            turn(columns[q][side * HALF + h * quarter : side * HALF + (h + 1) * quarter], NY * (q + 4 * h) - far)
+            for h in range(2)
+            for q in range(4)
+        ],
+        lane,
+        NY,
+    )
+    return wide_part, thin_part
+
+
+def halo_kernel(odd_ref, r_ref, first_ref, second_ref):
     owners = r_ref.shape[0] // 2
     cells = r_ref.shape[3]
-    lower = lax.broadcasted_iota(jnp.int32, (POINTS, cells), 1) < cells // 2
-    for pair in range(2):
-        first, second = (
-            r_ref[owners:, 2 * pair + part].reshape(POINTS, cells) for part in range(2)
-        )
-        up_ref[pair] = jnp.where(lower, pltpu.roll(first, cells // 2, 1), second)
-        first, second = (
-            r_ref[:owners, 2 * pair + part].reshape(POINTS, cells) for part in range(2)
-        )
-        down_ref[pair] = jnp.where(lower, first, pltpu.roll(second, cells // 2, 1))
+    odd = odd_ref[0] == 1
+    up = pack(r_ref.at[owners:], cells - 2 * NY, cells - 3 * NY, 1)
+    down = pack(r_ref.at[:owners], 0, 2 * NY, 0)
+    at = 0
+    for upper, lower in zip(up, down):
+        rows = upper.shape[0]
+        first_ref[at : at + rows, :] = jnp.where(odd, lower, upper)
+        second_ref[at : at + rows, :] = jnp.where(odd, upper, lower)
+        at += rows
 
 
 def load_columns(r_ref, x_ref):
@@ -194,10 +224,10 @@
             x_ref[POINTS : 2 * POINTS, at : at + cells] = low
 
 
-def spectral_kernel(damp_ref, r_ref, table_ref, symbol_ref, x_ref, y_ref):
+def middle_kernel(damp_ref, r_ref, forward_ref, symbol_ref, inverse_ref, inner_ref, out_ref, x_ref, y_ref):
     load_columns(r_ref, x_ref)
-    spectrum = dot(table_ref[:, : 2 * POINTS], x_ref[...]) + dot(
-        table_ref[:, 2 * POINTS :], x_ref[0:POINTS, :]
+    spectrum = dot(forward_ref[:, : 2 * POINTS], x_ref[...]) + dot(
+        forward_ref[:, 2 * POINTS :], x_ref[0:POINTS, :]
     )
     width = spectrum.shape[1] // 4
     row = lax.broadcasted_iota(jnp.int32, (HALF, width), 0)
@@ -229,66 +259,135 @@
             at = q * width
             y_ref[half * HALF : (half + 1) * HALF, at : at + width] = high
             y_ref[POINTS + half * HALF : POINTS + (half + 1) * HALF, at : at + width] = low
-
-
-def combine_kernel(x_ref, y_ref, before_ref, after_ref, table_ref, inner_ref, halo_ref, out_ref):
-    width = x_ref.shape[1] // 4
     cells = width // 2
     owners = out_ref.shape[0] // 2
     result = (
-        dot(table_ref[:, : 2 * POINTS], y_ref[...])
-        + dot(table_ref[:, 2 * POINTS : 3 * POINTS], y_ref[0:POINTS, :])
-        + dot(table_ref[:, 3 * POINTS :], x_ref[...])
-    )
-    halos = []
-    for pair in range(2):
-        before_high, before_low = split(before_ref[pair])
-        after_high, after_low = split(after_ref[pair])
-        halos.append(
-            (
-                jnp.concatenate([before_high, after_high], axis=1),
-                jnp.concatenate([before_low, after_low], axis=1),
+        dot(inverse_ref[:, : 2 * POINTS], y_ref[...])
+        + dot(inverse_ref[:, 2 * POINTS : 3 * POINTS], y_ref[0:POINTS, :])
+        + dot(inverse_ref[:, 3 * POINTS :], x_ref[...])
+    )
+    for side in range(2):
+        part = slice(side * HALF, (side + 1) * HALF)
+        low_part = slice(POINTS + side * HALF, POINTS + (side + 1) * HALF)
+        moved = sum(
+            dot(
+                jnp.concatenate(
+                    [x_ref[rows, q * width : (q + 1) * width] for q in range(4)], axis=0
+                ),
+                inner_ref[side],
             )
+            for rows in (part, low_part)
         )
-    for q in range(4):
-        columns = slice(q * width, (q + 1) * width)
-        for side in range(2):
-            part = slice(side * HALF, (side + 1) * HALF)
-            low = slice(POINTS + side * HALF, POINTS + (side + 1) * HALF)
-            inner, halo = inner_ref[side], halo_ref[side, q % 2]
-            high_halo, low_halo = halos[q // 2]
-            moved = (
-                dot(x_ref[part, columns], inner)
-                + dot(x_ref[low, columns], inner)
-                + dot(high_halo[part], halo)
-                + dot(low_halo[part], halo)
+        speed = speed_over_60(side * HALF, HALF, width)
+        rows = owners // 2
+        for q in range(4):
+            value = (
+                result[part, q * width : (q + 1) * width]
+                - moved[q * HALF : (q + 1) * HALF] * speed
             )
-            value = result[part, columns] - moved * speed_over_60(side * HALF, HALF, width)
-            rows = owners // 2
             for band in range(2):
                 out_ref[
                     band * owners + side * rows : band * owners + (side + 1) * rows, q
                 ] = value[:, band * cells : (band + 1) * cells].reshape(rows, -1, cells)
 
 
+def lane_weight(lane, first_row, last_row, weight):
+    return jnp.where((lane >= first_row * NY) & (lane < last_row * NY), weight, 0.0)
+
+
+def edge_kernel(odd_ref, partial_ref, first_ref, second_ref, out_ref):
+    owners = out_ref.shape[0] // 2
+    cells = out_ref.shape[3]
+    odd = odd_ref[0] == 1
+    band_rows = cells // NY
+    quarter = HALF // 2
+    half_owners = owners // 2
+    lane = lax.broadcasted_iota(jnp.int32, (HALF, cells), 1)
+
+    def both(rows):
+        return first_ref[rows, :], second_ref[rows, :]
+
+    thin_first, thin_second = both(slice(POINTS, POINTS + quarter))
+    for side, stencil in enumerate((PLUS, MINUS)):
+        weights = dict(stencil)
+        one, two = both(slice(side * HALF, (side + 1) * HALF))
+        before, after = jnp.where(odd, one, two), jnp.where(odd, two, one)
+        if side:
+            thin = jnp.where(odd, thin_first, thin_second)
+        else:
+            thin = jnp.where(odd, thin_second, thin_first)
+        speed = speed_over_60(side * HALF, HALF, cells)
+        low = slice(side * half_owners, (side + 1) * half_owners)
+        high = slice(owners + side * half_owners, owners + (side + 1) * half_owners)
+        for q in range(4):
+            moved_low = moved_high = 0.0
+            for s in range(1, 4 if side else 3):
+                moved_low += lane_weight(lane, max(s - 2, 0), s, weights[-s]) * turn(
+                    before, NY * (s - 2 - 2 * q)
+                )
+            for s in range(1, 3 if side else 4):
+                top = band_rows - s
+                moved_high += lane_weight(
+                    lane, top, min(top + 2, band_rows), weights[s]
+                ) * turn(after, NY * (top - 2 * q))
+            third = jnp.concatenate(
+                [
+                    turn(thin, NY * ((0 if side else band_rows - 1) - q - 4 * h))
+                    for h in range(2)
+                ],
+                axis=0,
+            )
+            if side:
+                moved_low += lane_weight(lane, 0, 1, weights[-3]) * third
+            else:
+                moved_high += lane_weight(lane, band_rows - 1, band_rows, weights[3]) * third
+            out_ref[low, q] = partial_ref[low, q] - (moved_low * speed).reshape(
+                half_owners, -1, cells
+            )
+            out_ref[high, q] = partial_ref[high, q] - (moved_high * speed).reshape(
+                half_owners, -1, cells
+            )
+
+
 VMEM_SPEC = pl.BlockSpec(memory_space=pltpu.VMEM)
 SMEM_SPEC = pl.BlockSpec(memory_space=pltpu.SMEM)
 
 
-def call(kernel, shapes, inputs, scratch=(), flops=1, smem=0, name=None):
+def on_chip(value):
+    return pltpu.with_memory_space_constraint(value, pltpu.VMEM)
+
+
+def call(
+    kernel,
+    shapes,
+    inputs,
+    scratch=(),
+    flops=1,
+    smem=0,
+    keep=True,
+    grid=(),
+    in_specs=None,
+    out_specs=None,
+):
     bytes_accessed = sum(v.size * v.dtype.itemsize for v in inputs)
-    shapes = [jax.ShapeDtypeStruct(*s) for s in shapes]
+    shapes = [pltpu.VMEM(*s) if keep else jax.ShapeDtypeStruct(*s) for s in shapes]
+    if in_specs is None:
+        inputs = [*inputs[:smem], *(on_chip(v) for v in inputs[smem:])]
+        in_specs = [SMEM_SPEC] * smem + [VMEM_SPEC] * (len(inputs) - smem)
+    if out_specs is None:
+        out_specs = [VMEM_SPEC] * len(shapes)
     single = len(shapes) == 1
     return pl.pallas_call(
         kernel,
+        grid=grid,
         out_shape=shapes[0] if single else shapes,
-        in_specs=[SMEM_SPEC] * smem + [VMEM_SPEC] * (len(inputs) - smem),
-        out_specs=VMEM_SPEC if single else [VMEM_SPEC] * len(shapes),
+        in_specs=in_specs,
+        out_specs=out_specs[0] if single else out_specs,
         scratch_shapes=list(scratch),
         cost_estimate=pl.CostEstimate(
             flops=flops, bytes_accessed=2 * bytes_accessed, transcendentals=0
         ),
-        name=name,
+        compiler_params=pltpu.CompilerParams(vmem_limit_bytes=24 << 20),
     )(*inputs)
 
 
@@ -338,16 +437,20 @@
     return symbol, damp
 
 
-def stage_forward(density, table):
+def stage_forward(density, table, keep=SENT_ON_CHIP):
     planes, points, cells = density.shape
-    width = planes * cells
     sent = call(
         forward_kernel,
         [((points * planes, cells), F32)],
         (density, table["forward_second"]),
-        (pltpu.VMEM((2 * points, width), BF16),),
-        6 * points * points * width,
-        name="forward_second",
+        flops=6 * points * points * planes * cells,
+        keep=keep,
+        grid=(FORWARD_STEPS,),
+        in_specs=[
+            pl.BlockSpec((planes // FORWARD_STEPS, points, cells), lambda i: (i, 0, 0)),
+            pl.BlockSpec((points, 3 * points), lambda i: (0, 0)),
+        ],
+        out_specs=[VMEM_SPEC if keep else pl.BlockSpec((points * planes, cells), lambda i: (0, 0))],
     )
     return sent.reshape(points // 4, 4, planes, cells)
 
@@ -359,58 +462,72 @@
         [((planes, points, cells), F32)],
         (density, table["friction"], table["column_shift"]),
         flops=6 * points * points * planes * cells,
-        name="local_part",
-    )
-
-
-def stage_halo(columns):
+    )
+
+
+def stage_halo(odd, columns):
     cells = columns.shape[3]
     return call(
-        halo_kernel, [((2, POINTS, cells), F32)] * 2, (columns,), name="halo_pack"
-    )
-
-
-def stage_spectral(damp, columns, symbol, table):
-    width = 8 * columns.shape[3]
+        halo_kernel, [((POINTS + POINTS // 4, cells), F32)] * 2, (odd, columns), smem=1
+    )
+
+
+def stage_middle(damp, columns, symbol, table):
+    _, _, _, cells = columns.shape
+    width = 8 * cells
+    scratch = pltpu.VMEM((2 * POINTS, width), BF16)
     return call(
-        spectral_kernel,
-        [((2 * POINTS, width), BF16)] * 2,
-        (damp, columns, table["forward_first"], symbol),
-        flops=6 * POINTS * POINTS * width,
+        middle_kernel,
+        [(columns.shape, F32)],
+        (
+            damp,
+            columns,
+            table["forward_first"],
+            symbol,
+            table["inverse_first"],
+            table["row_inner"],
+        ),
+        (scratch, scratch),
+        20 * POINTS * POINTS * width,
         smem=1,
-        name="spectral",
-    )
-
-
-def stage_combine(x, y, before, after, table, planes, members):
-    width = x.shape[1]
+    )
+
+
+def stage_edge(odd, partial, first, second, keep=SENT_ON_CHIP):
     return call(
-        combine_kernel,
-        [((members, 4, planes, width // 8), F32)],
-        (x, y, before, after, table["inverse_first"], table["row_inner"], table["row_halo"]),
-        flops=18 * POINTS * POINTS * width,
-        name="combine",
+        edge_kernel,
+        [(partial.shape, F32)],
+        (odd, partial, first, second),
+        flops=40 * partial.size,
+        smem=1,
+        keep=keep,
     )
 
 
 def stage_backward(panels, here, table):
     planes, points, cells = here.shape
-    width = planes * cells
     return call(
         backward_kernel,
         [((planes, points, cells), F32)],
-        (panels.reshape(points * planes, cells), here, table["inverse_second"]),
-        (pltpu.VMEM((2 * points, width), BF16),),
-        6 * points * points * width,
-        name="inverse_second",
+        (
+            on_chip(panels.reshape(points * planes, cells)),
+            on_chip(here),
+            on_chip(table["inverse_second"]),
+        ),
+        flops=6 * points * points * planes * cells,
+        keep=False,
+        grid=(BACKWARD_STEPS,),
+        in_specs=[VMEM_SPEC] * 3,
+        out_specs=[
+            pl.BlockSpec((planes // BACKWARD_STEPS, points, cells), lambda i: (i, 0, 0))
+        ],
     )
 
 
 def local(density, mode_waves, mode_amplitudes, mode_phases):
-    planes, _, cells = density.shape
+    _, _, cells = density.shape
     rows_dev = cells // NY
     group = ("pair", "mom")
-    members = lax.axis_size(group)
     strips = lax.axis_size("y")
     table = tables(rows_dev)
 
@@ -418,6 +535,7 @@
     columns = lax.all_to_all(sent, group, split_axis=0, concat_axis=0, tiled=True)
     here = stage_local(density, table)
     position = lax.axis_index("pair") * lax.axis_size("mom") + lax.axis_index("mom")
+    odd = (lax.axis_index("y") % 2).reshape(1)
     symbol, damp = symbol_table(
         mode_waves,
         mode_amplitudes,
@@ -427,11 +545,13 @@
         2 * rows_dev,
         2 * rows_dev * strips,
     )
-    up, down = stage_halo(columns)
-    before = lax.ppermute(up, "y", [(i, (i + 1) % strips) for i in range(strips)])
-    after = lax.ppermute(down, "y", [((i + 1) % strips, i) for i in range(strips)])
-    x, y = stage_spectral(damp, columns, symbol, table)
-    back = stage_combine(x, y, before, after, table, planes, members)
+    first, second = stage_halo(odd, columns)
+    links = [(i, (i + 1) % strips) for i in range(strips)]
+    swaps = [[p for l in links[start::2] for p in (l, l[::-1])] for start in range(2)]
+    first = lax.ppermute(first, "y", swaps[0])
+    second = lax.ppermute(second, "y", swaps[1])
+    partial = stage_middle(damp, columns, symbol, table)
+    back = stage_edge(odd, partial, first, second)
     panels = lax.all_to_all(back, group, split_axis=0, concat_axis=0, tiled=True)
     return stage_backward(panels, here, table)
 

time: 109 us -> 99.4 us (0.912)
  the two profiles are of different devices: /device:TPU:24 before, /device:TPU:1 now
where the time goes in v1:
time: 99.4 us; the launch traced here: 98.8 us
  waiting for transfers between devices  50.5 us (51%)
  starting transfers between devices  29.9 us (30%)
  Pallas kernels  9.17 us (9%)
  local copies, waits for them, and re-layouts  7.46 us (8%)
  matrix products  1.12 us (1%)
    all_to_all x1, waiting for transfers between devices, local(): lax.all_to_all(back, group, split_axis=0, concat_axis=0, tiled=True)  25.3 us
    all_to_all x1, waiting for transfers between devices, local(): lax.all_to_all(sent, group, split_axis=0, concat_axis=0, tiled=True)  25.2 us
    all_to_all x1, starting transfers between devices, local(): lax.all_to_all(sent, group, split_axis=0, concat_axis=0, tiled=True)  14.8 us
    pallas_call x6, Pallas kernels, call(): pl.pallas_call(kernel, grid=grid, out_shape=shapes[0] if single else shap...  9.17 us
    unnamed x24, local copies, waits for them, and re-layouts  7.37 us
    all_to_all x1, starting transfers between devices, local(): lax.all_to_all(back, group, split_axis=0, concat_axis=0, tiled=True)  6.96 us
    ppermute x1, starting transfers between devices, local(): second = lax.ppermute(second, 'y', swaps[1])  4.87 us
    ppermute x1, starting transfers between devices, local(): first = lax.ppermute(first, 'y', swaps[0])  3.21 us
  transfers between devices with their start and end apart: 4, of which 2 were waited for; matrix products, arithmetic and copies ran while one was open for 2% of the time, Pallas kernels for 3%

profile of v1, /device:TPU:1, one launch (start us, length us, event | category | flops | bytes accessed | tf_op | source)
XLA Modules:
  0.0 98.8 jit_solution(17096624822016529032)
XLA Ops:
  0.0 1.2 %copy-done = f32[8,256,128]{2,1,0:T(8,128)S(1)} copy-done((f32[8,256,128]{2,1,0:T(8,128)S(1)}, f32[8,256,128]{2,1,0:T(8,128)}, u32[]{:S(2)}) %copy-start) | copy-done | bytes 1048600
  1.2 1.0 %copy-done.3 = bf16[256,768]{1,0:T(8,128)(2,1)S(1)} copy-done((bf16[256,768]{1,0:T(8,128)(2,1)S(1)}, bf16[256,768]{1,0:T(8,128)(2,1)}, u32[]{:S(2)}) %copy-start.3) | copy-done | bytes 393240
  2.2 2.1 %shard_map.109 = f32[2048,128]{1,0:T(8,128)} custom-call(f32[8,256,128]{2,1,0:T(8,128)S(1)} %copy-done, bf16[256,768]{1,0:T(8,128)(2,1)S(1)} %copy-done.3), custom_call_target="tpu_custom_call" | custom-call | flops 402653184 | bytes 2883584 | tf_op jit(solution)/shard_map/pallas_call | solution.py:380
  4.3 14.8 %all-to-all-start = ((f32[64,4,8,128]{3,2,1,0:T(8,128)}), f32[64,4,8,128]{3,2,1,0:T(8,128)S(1)}, u32[]{:S(2)}, u32[]{:S(2)}) async-start(f32[64,4,8,128]{3,2,1,0:T(8,128)} %bitcast.1), calls=%async_computation | async-start | bytes 2097152 | tf_op jit(solution)/shard_map/all_to_all | solution.py:535
  19.2 0.7 copy-done.9
  19.9 0.1 fusion.68
  20.0 0.1 fusion.53
  20.3 0.7 copy-done.10
  21.0 1.1 %fusion.symbol_ref = f32[2,4,128,256]{3,2,1,0:T(8,128)S(1)} fusion(f32[2,1,128,16]{2,3,1,0:T(8,128)S(1)} %get-tuple-element.14, f32[2,1,128,16]{2,3,1,0:T(8,128)S(1)} %get-tuple-element.13, f32[2,1,128,16]{2,3,1,0:T(8,128)S(1)} %get-tuple-element.10, f32[2,1,128,16]{2,3,1,0:T(8,128)S(1)} %get-tuple-element.9, f32[16]{0:T(128)S(1)} %copy-done.10, ...), kind=kOutput, calls=%fused_computation | convolution fusion | flops 50511872 | bytes 1116416 | tf_op jit(solution)/shard_map/dot_general | solution.py:431
  22.1 25.2 %all-to-all-done.r_ref = f32[64,4,8,128]{3,2,1,0:T(8,128)S(1)} async-done(((f32[64,4,8,128]{3,2,1,0:T(8,128)}), f32[64,4,8,128]{3,2,1,0:T(8,128)S(1)}, u32[]{:S(2)}, u32[]{:S(2)}) %all-to-all-start) | async-done | bytes 1048608 | tf_op jit(solution)/shard_map/all_to_all | solution.py:535
  47.3 0.4 shard_map.111
  47.7 3.2 %collective-permute-start = (f32[320,128]{1,0:T(8,128)S(1)}, f32[320,128]{1,0:T(8,128)S(1)}, u32[]{:S(2)}, u32[]{:S(2)}) collective-permute-start(f32[320,128]{1,0:T(8,128)S(1)} %get-tuple-element.7), channel_id=1, source_target_pairs={{0,64},{64,0},{128,192},{192,128},{256,320},{320,256},{384,448},{4... | collective-permute-start | bytes 491528 | tf_op jit(solution)/shard_map/ppermute | solution.py:551
  50.9 4.9 %collective-permute-start.1 = (f32[320,128]{1,0:T(8,128)S(1)}, f32[320,128]{1,0:T(8,128)S(1)}, u32[]{:S(2)}, u32[]{:S(2)}) collective-permute-start(f32[320,128]{1,0:T(8,128)S(1)} %get-tuple-element.8), channel_id=1, source_target_pairs={{64,128},{128,64},{192,256},{256,192},{320,384},{384,320},{448,0},... | collective-permute-start | bytes 491528 | tf_op jit(solution)/shard_map/ppermute | solution.py:552
  55.8 0.1 mul.283.damp_ref
  55.9 1.0 %copy-done.7 = bf16[256,768]{1,0:T(8,128)(2,1)S(1)} copy-done((bf16[256,768]{1,0:T(8,128)(2,1)S(1)}, bf16[256,768]{1,0:T(8,128)(2,1)}, u32[]{:S(2)}) %copy-start.7) | copy-done | bytes 393240
  56.9 0.9 copy-done.8
  57.9 2.4 %shard_map.110.partial_ref = f32[64,4,8,128]{3,2,1,0:T(8,128)S(1)} custom-call(f32[4]{0:T(128)S(1)} %mul.283.damp_ref, f32[64,4,8,128]{3,2,1,0:T(8,128)S(1)} %all-to-all-done.r_ref, bf16[256,768]{1,0:T(8,128)(2,1)S(1)} %copy-done.7, f32[2,4,128,256]{3,2,1,0:T(8,128)S(1)} %fusion.symbol_ref, bf16[256,1280]{1,0:T(8,128)(2,1)S(1)} %copy-done.6, ...), custom_call_target="tpu_custom_call" | custom-call | flops 1342177280 | bytes 6815776 | tf_op jit(solution)/shard_map/pallas_call | solution.py:380
  60.3 1.7 %shard_map.112 = f32[64,4,8,128]{3,2,1,0:T(8,128)} custom-call(s32[1]{0:T(128)} %bitcast.odd_ref, f32[64,4,8,128]{3,2,1,0:T(8,128)S(1)} %shard_map.110.partial_ref, f32[320,128]{1,0:T(8,128)S(1)} %collective-permute-done.first_ref, f32[320,128]{1,0:T(8,128)S(1)} %collective-permute-done.1.second_ref), custom_call_target="tpu_custom_call" | custom-call | flops 10485760 | bytes 2752520 | tf_op jit(solution)/shard_map/pallas_call | solution.py:380
  62.0 7.0 %all-to-all-start.1 = ((f32[64,4,8,128]{3,2,1,0:T(8,128)}), f32[64,4,8,128]{3,2,1,0:T(8,128)S(1)}, u32[]{:S(2)}, u32[]{:S(2)}) async-start(f32[64,4,8,128]{3,2,1,0:T(8,128)} %shard_map.112), calls=%async_computation.1 | async-start | bytes 2097152 | tf_op jit(solution)/shard_map/all_to_all | solution.py:555
  69.0 0.9 copy-done.4
  69.9 0.9 copy-done.5
  70.8 1.0 shard_map.113.local_ref
  71.8 25.3 %all-to-all-done.1 = f32[64,4,8,128]{3,2,1,0:T(8,128)S(1)} async-done(((f32[64,4,8,128]{3,2,1,0:T(8,128)}), f32[64,4,8,128]{3,2,1,0:T(8,128)S(1)}, u32[]{:S(2)}, u32[]{:S(2)}) %all-to-all-start.1) | async-done | bytes 1048608 | tf_op jit(solution)/shard_map/all_to_all | solution.py:555
  97.1 1.7 %shard_map.114 = f32[8,256,128]{2,1,0:T(8,128)} custom-call(f32[2048,128]{1,0:T(8,128)S(1)} %bitcast.14, f32[8,256,128]{2,1,0:T(8,128)S(1)} %shard_map.113.local_ref, bf16[256,768]{1,0:T(8,128)(2,1)S(1)} %copy-done.2), custom_call_target="tpu_custom_call" | custom-call | flops 402653184 | bytes 4980736 | tf_op jit(solution)/shard_map/pallas_call | solution.py:380
  (26 shorter events, 0.3 us)
Async XLA Ops:
  0.0 1.2 %copy-start = (f32[8,256,128]{2,1,0:T(8,128)S(1)}, f32[8,256,128]{2,1,0:T(8,128)}, u32[]{:S(2)}) copy-start(f32[8,256,128]{2,1,0:T(8,128)} %u_ref.3) | copy-start | bytes 3145732
  1.2 1.0 %copy-start.3 = (bf16[256,768]{1,0:T(8,128)(2,1)S(1)}, bf16[256,768]{1,0:T(8,128)(2,1)}, u32[]{:S(2)}) copy-start(bf16[256,768]{1,0:T(8,128)(2,1)} %constant.145.clone.table_ref) | copy-start | bytes 1179652
  4.3 43.0 %all-to-all-start = ((f32[64,4,8,128]{3,2,1,0:T(8,128)}), f32[64,4,8,128]{3,2,1,0:T(8,128)S(1)}, u32[]{:S(2)}, u32[]{:S(2)}) async-start(f32[64,4,8,128]{3,2,1,0:T(8,128)} %bitcast.1), calls=%async_computation | async-start | bytes 2097152 | tf_op jit(solution)/shard_map/all_to_all | solution.py:535
  19.2 0.7 copy-start.9
  20.3 0.7 copy-start.10
  20.3 0.7 copy-start.11
  22.1 33.8 %copy-start.6 = (bf16[256,1280]{1,0:T(8,128)(2,1)S(1)}, bf16[256,1280]{1,0:T(8,128)(2,1)}, u32[]{:S(2)}) copy-start(bf16[256,1280]{1,0:T(8,128)(2,1)} %constant.148.clone.inverse_ref) | copy-start | bytes 1966084
  47.7 12.6 %collective-permute-start = (f32[320,128]{1,0:T(8,128)S(1)}, f32[320,128]{1,0:T(8,128)S(1)}, u32[]{:S(2)}, u32[]{:S(2)}) collective-permute-start(f32[320,128]{1,0:T(8,128)S(1)} %get-tuple-element.7), channel_id=1, source_target_pairs={{0,64},{64,0},{128,192},{192,128},{256,320},{320,256},{384,448},{4... | collective-permute-start | bytes 491528 | tf_op jit(solution)/shard_map/ppermute | solution.py:551
  50.9 9.4 %collective-permute-start.1 = (f32[320,128]{1,0:T(8,128)S(1)}, f32[320,128]{1,0:T(8,128)S(1)}, u32[]{:S(2)}, u32[]{:S(2)}) collective-permute-start(f32[320,128]{1,0:T(8,128)S(1)} %get-tuple-element.8), channel_id=1, source_target_pairs={{64,128},{128,64},{192,256},{256,192},{320,384},{384,320},{448,0},... | collective-permute-start | bytes 491528 | tf_op jit(solution)/shard_map/ppermute | solution.py:552
  55.9 1.0 %copy-start.7 = (bf16[256,768]{1,0:T(8,128)(2,1)S(1)}, bf16[256,768]{1,0:T(8,128)(2,1)}, u32[]{:S(2)}) copy-start(bf16[256,768]{1,0:T(8,128)(2,1)} %constant.147.clone.forward_ref) | copy-start | bytes 1179652
  56.9 0.9 copy-start.8
  62.0 7.0 %copy-start.1 = (f32[8,256,128]{2,1,0:T(8,128)S(1)}, f32[8,256,128]{2,1,0:T(8,128)}, u32[]{:S(2)}) copy-start(f32[8,256,128]{2,1,0:T(8,128)} %u_ref.3) | copy-start | bytes 3145732
  62.0 35.1 %all-to-all-start.1 = ((f32[64,4,8,128]{3,2,1,0:T(8,128)}), f32[64,4,8,128]{3,2,1,0:T(8,128)S(1)}, u32[]{:S(2)}, u32[]{:S(2)}) async-start(f32[64,4,8,128]{3,2,1,0:T(8,128)} %shard_map.112), calls=%async_computation.1 | async-start | bytes 2097152 | tf_op jit(solution)/shard_map/all_to_all | solution.py:555
  69.0 1.0 copy-start.4
  69.9 0.9 copy-start.5
  70.8 26.3 %copy-start.2 = (bf16[256,768]{1,0:T(8,128)(2,1)S(1)}, bf16[256,768]{1,0:T(8,128)(2,1)}, u32[]{:S(2)}) copy-start(bf16[256,768]{1,0:T(8,128)(2,1)} %constant.146.clone.table_ref) | copy-start | bytes 1179652

commit v2 on v1

--- a/solution.py
+++ b/solution.py
@@ -21,13 +21,12 @@
 HIGHEST_PRECISION = lax.Precision.HIGHEST
 FORWARD_STEPS = 4
 BACKWARD_STEPS = 2
-SENT_ON_CHIP = True
 
 
 def wide(table):
     high = table.astype(ml_dtypes.bfloat16)
     low = (table - high.astype(np.float64)).astype(ml_dtypes.bfloat16)
-    return np.concatenate([high, high, low], axis=1)
+    return np.concatenate([high, low], axis=1)
 
 
 def real_fourier():
@@ -88,7 +87,7 @@
     result["forward_first"] = jnp.asarray(wide(forward))
     friction = friction_matrix().astype(ml_dtypes.bfloat16)
     result["inverse_first"] = jnp.asarray(
-        np.concatenate([wide(inverse), friction, friction], axis=1)
+        np.concatenate([wide(inverse), friction], axis=1)
     )
     result["friction"] = jnp.asarray(np.concatenate([friction, friction], axis=1))
     rows = 2 * rows_dev
@@ -116,6 +115,14 @@
     return jnp.dot(left, right, preferred_element_type=F32)
 
 
+def wide_dot(table, high, low):
+    return (
+        dot(table[:, :POINTS], high)
+        + dot(table[:, :POINTS], low)
+        + dot(table[:, POINTS : 2 * POINTS], high)
+    )
+
+
 def speed_over_60(first, count, width):
     index = first + lax.broadcasted_iota(jnp.int32, (count, width), 0)
     return (2 * index - (POINTS - 1)).astype(F32) * (1.0 / (60 * POINTS))
@@ -126,9 +133,7 @@
     first = pl.program_id(0) * planes
     parts = [split(u_ref[k]) for k in range(planes)]
     high, low = (jnp.concatenate(values, axis=1) for values in zip(*parts))
-    result = dot(table_ref[:, : 2 * POINTS], jnp.concatenate([high, low], axis=0)) + dot(
-        table_ref[:, 2 * POINTS :], high
-    )
+    result = wide_dot(table_ref[...], high, low)
     stride = out_ref.shape[0] // POINTS
     for k in range(planes):
         out_ref[pl.ds(first + k, POINTS, stride=stride), :] = result[
@@ -144,9 +149,7 @@
         split(w_ref[pl.ds(first + k, POINTS, stride=stride), :]) for k in range(planes)
     ]
     high, low = (jnp.concatenate(values, axis=1) for values in zip(*parts))
-    result = dot(table_ref[:, : 2 * POINTS], jnp.concatenate([high, low], axis=0)) + dot(
-        table_ref[:, 2 * POINTS :], high
-    )
+    result = wide_dot(table_ref[...], high, low)
     for k in range(planes):
         out_ref[k] = result[:, k * cells : (k + 1) * cells] + local_ref[first + k]
 
@@ -226,9 +229,7 @@
 
 def middle_kernel(damp_ref, r_ref, forward_ref, symbol_ref, inverse_ref, inner_ref, out_ref, x_ref, y_ref):
     load_columns(r_ref, x_ref)
-    spectrum = dot(forward_ref[:, : 2 * POINTS], x_ref[...]) + dot(
-        forward_ref[:, 2 * POINTS :], x_ref[0:POINTS, :]
-    )
+    spectrum = wide_dot(forward_ref[...], x_ref[0:POINTS, :], x_ref[POINTS:, :])
     width = spectrum.shape[1] // 4
     row = lax.broadcasted_iota(jnp.int32, (HALF, width), 0)
     scale = DAMPING / (HALF * HALF)
@@ -261,10 +262,12 @@
             y_ref[POINTS + half * HALF : POINTS + (half + 1) * HALF, at : at + width] = low
     cells = width // 2
     owners = out_ref.shape[0] // 2
+    inverse = inverse_ref[...]
+    friction = inverse[:, 2 * POINTS :]
     result = (
-        dot(inverse_ref[:, : 2 * POINTS], y_ref[...])
-        + dot(inverse_ref[:, 2 * POINTS : 3 * POINTS], y_ref[0:POINTS, :])
-        + dot(inverse_ref[:, 3 * POINTS :], x_ref[...])
+        wide_dot(inverse, y_ref[0:POINTS, :], y_ref[POINTS:, :])
+        + dot(friction, x_ref[0:POINTS, :])
+        + dot(friction, x_ref[POINTS:, :])
     )
     for side in range(2):
         part = slice(side * HALF, (side + 1) * HALF)
@@ -296,57 +299,48 @@
 
 
 def edge_kernel(odd_ref, partial_ref, first_ref, second_ref, out_ref):
-    owners = out_ref.shape[0] // 2
-    cells = out_ref.shape[3]
-    odd = odd_ref[0] == 1
+    for step in range(4):
+        pl.when(pl.program_id(0) == step)(
+            lambda step=step: edge_part(
+                step // 2, step % 2, odd_ref, partial_ref, first_ref, second_ref, out_ref
+            )
+        )
+
+
+def edge_part(band, side, odd_ref, partial_ref, first_ref, second_ref, out_ref):
+    owners, _, _, cells = out_ref.shape
     band_rows = cells // NY
-    quarter = HALF // 2
-    half_owners = owners // 2
+    stencil = dict((PLUS, MINUS)[side])
+    weights = [stencil.get(s if band else -s) for s in (1, 2, 3)]
+    odd = (odd_ref[0] == 1) != bool(band)
     lane = lax.broadcasted_iota(jnp.int32, (HALF, cells), 1)
 
-    def both(rows):
-        return first_ref[rows, :], second_ref[rows, :]
-
-    thin_first, thin_second = both(slice(POINTS, POINTS + quarter))
-    for side, stencil in enumerate((PLUS, MINUS)):
-        weights = dict(stencil)
-        one, two = both(slice(side * HALF, (side + 1) * HALF))
-        before, after = jnp.where(odd, one, two), jnp.where(odd, two, one)
-        if side:
-            thin = jnp.where(odd, thin_first, thin_second)
-        else:
-            thin = jnp.where(odd, thin_second, thin_first)
-        speed = speed_over_60(side * HALF, HALF, cells)
-        low = slice(side * half_owners, (side + 1) * half_owners)
-        high = slice(owners + side * half_owners, owners + (side + 1) * half_owners)
-        for q in range(4):
-            moved_low = moved_high = 0.0
-            for s in range(1, 4 if side else 3):
-                moved_low += lane_weight(lane, max(s - 2, 0), s, weights[-s]) * turn(
-                    before, NY * (s - 2 - 2 * q)
-                )
-            for s in range(1, 3 if side else 4):
-                top = band_rows - s
-                moved_high += lane_weight(
-                    lane, top, min(top + 2, band_rows), weights[s]
-                ) * turn(after, NY * (top - 2 * q))
+    def received(rows):
+        return jnp.where(odd, first_ref[rows, :], second_ref[rows, :])
+
+    pair = received(slice(side * HALF, (side + 1) * HALF))
+    thin = received(slice(POINTS, POINTS + HALF // 2)) if weights[2] else None
+    speed = speed_over_60(side * HALF, HALF, cells)
+    block = slice((2 * band + side) * owners, (2 * band + side + 1) * owners)
+    for q in range(4):
+        moved = 0.0
+        for s, weight in enumerate(weights, 1):
+            if weight is None:
+                continue
+            if band:
+                near = band_rows - s
+                rows = (near, min(near + 2, band_rows))
+            else:
+                near = s - 2
+                rows = (max(near, 0), s)
+            moved += lane_weight(lane, *rows, weight) * turn(pair, NY * (near - 2 * q))
+        if thin is not None:
+            row = band_rows - 1 if band else 0
             third = jnp.concatenate(
-                [
-                    turn(thin, NY * ((0 if side else band_rows - 1) - q - 4 * h))
-                    for h in range(2)
-                ],
-                axis=0,
+                [turn(thin, NY * (row - q - 4 * h)) for h in range(2)], axis=0
             )
-            if side:
-                moved_low += lane_weight(lane, 0, 1, weights[-3]) * third
-            else:
-                moved_high += lane_weight(lane, band_rows - 1, band_rows, weights[3]) * third
-            out_ref[low, q] = partial_ref[low, q] - (moved_low * speed).reshape(
-                half_owners, -1, cells
-            )
-            out_ref[high, q] = partial_ref[high, q] - (moved_high * speed).reshape(
-                half_owners, -1, cells
-            )
+            moved += lane_weight(lane, row, row + 1, weights[2]) * third
+        out_ref[:, q] = partial_ref[block, q] - (moved * speed).reshape(owners, -1, cells)
 
 
 VMEM_SPEC = pl.BlockSpec(memory_space=pltpu.VMEM)
@@ -437,20 +431,24 @@
     return symbol, damp
 
 
-def stage_forward(density, table, keep=SENT_ON_CHIP):
+def off_chip(value):
+    return pltpu.with_memory_space_constraint(value, pltpu.HBM)
+
+
+def stage_forward(density, table):
     planes, points, cells = density.shape
     sent = call(
         forward_kernel,
         [((points * planes, cells), F32)],
-        (density, table["forward_second"]),
+        (off_chip(density), off_chip(table["forward_second"])),
         flops=6 * points * points * planes * cells,
-        keep=keep,
+        keep=False,
         grid=(FORWARD_STEPS,),
         in_specs=[
             pl.BlockSpec((planes // FORWARD_STEPS, points, cells), lambda i: (i, 0, 0)),
-            pl.BlockSpec((points, 3 * points), lambda i: (0, 0)),
+            pl.BlockSpec((points, 2 * points), lambda i: (0, 0)),
         ],
-        out_specs=[VMEM_SPEC if keep else pl.BlockSpec((points * planes, cells), lambda i: (0, 0))],
+        out_specs=[pl.BlockSpec((points * planes, cells), lambda i: (0, 0))],
     )
     return sent.reshape(points // 4, 4, planes, cells)
 
@@ -493,14 +491,17 @@
     )
 
 
-def stage_edge(odd, partial, first, second, keep=SENT_ON_CHIP):
+def stage_edge(odd, partial, first, second):
+    members, _, planes, cells = partial.shape
     return call(
         edge_kernel,
         [(partial.shape, F32)],
-        (odd, partial, first, second),
+        (odd, on_chip(partial), on_chip(first), on_chip(second)),
         flops=40 * partial.size,
-        smem=1,
-        keep=keep,
+        keep=False,
+        grid=(4,),
+        in_specs=[SMEM_SPEC] + [VMEM_SPEC] * 3,
+        out_specs=[pl.BlockSpec((members // 4, 4, planes, cells), lambda i: (i, 0, 0, 0))],
     )
 
 

time: 99.4 us -> 99.3 us (level)
  local copies, waits for them, and re-layouts: 7.46 us -> 3.35 us
  Pallas kernels: 9.17 us -> 11.5 us
  waiting for transfers between devices: 50.5 us -> 52.4 us
    unnamed x24 -> x20, local copies, waits for them, and re-layouts: 7.37 us -> 3.26 us
    pallas_call x6, Pallas kernels: 9.17 us -> 11.5 us  [call(): pl.pallas_call(kernel, grid=grid, out_shape=shapes[0] if single else shap...]
    all_to_all x1, waiting for transfers between devices: 25.3 us -> 27.2 us  [local(): lax.all_to_all(back, group, split_axis=0, concat_axis=0, tiled=True)]
  transfers between devices with their start and end apart: 4 -> 4, of which waited for: 2 -> 2; matrix products, arithmetic and copies ran while one was open for 2% -> 2% of each run, Pallas kernels for 3% -> 4%
where the time goes in v2:
time: 99.3 us; the launch traced here: 98.9 us
  waiting for transfers between devices  52.4 us (53%)
  starting transfers between devices  29.8 us (30%)
  Pallas kernels  11.5 us (12%)
  local copies, waits for them, and re-layouts  3.35 us (3%)
  matrix products  1.12 us (1%)
    all_to_all x1, waiting for transfers between devices, local(): lax.all_to_all(back, group, split_axis=0, concat_axis=0, tiled=True)  27.2 us
    all_to_all x1, waiting for transfers between devices, local(): lax.all_to_all(sent, group, split_axis=0, concat_axis=0, tiled=True)  25.2 us
    all_to_all x1, starting transfers between devices, local(): lax.all_to_all(sent, group, split_axis=0, concat_axis=0, tiled=True)  14.8 us
    pallas_call x6, Pallas kernels, call(): pl.pallas_call(kernel, grid=grid, out_shape=shapes[0] if single else shap...  11.5 us
    all_to_all x1, starting transfers between devices, local(): lax.all_to_all(back, group, split_axis=0, concat_axis=0, tiled=True)  6.95 us
    ppermute x1, starting transfers between devices, local(): second = lax.ppermute(second, 'y', swaps[1])  4.87 us
    unnamed x20, local copies, waits for them, and re-layouts  3.26 us
    ppermute x1, starting transfers between devices, local(): first = lax.ppermute(first, 'y', swaps[0])  3.21 us
  transfers between devices with their start and end apart: 4, of which 2 were waited for; matrix products, arithmetic and copies ran while one was open for 2% of the time, Pallas kernels for 4%

profile of v2, /device:TPU:1, one launch (start us, length us, event | category | flops | bytes accessed | tf_op | source)
XLA Modules:
  0.0 98.9 jit_solution(9651379807807382586)
XLA Ops:
  0.0 3.8 %shard_map.109 = f32[2048,128]{1,0:T(8,128)} custom-call(f32[8,256,128]{2,1,0:T(8,128)} %u_ref.3, bf16[256,512]{1,0:T(8,128)(2,1)} %constant.145.clone.table_ref), custom_call_target="tpu_custom_call" | custom-call | flops 402653184 | bytes 2621440 | tf_op jit(solution)/shard_map/pallas_call | solution.py:374
  3.8 14.8 %all-to-all-start = ((f32[64,4,8,128]{3,2,1,0:T(8,128)}), f32[64,4,8,128]{3,2,1,0:T(8,128)S(1)}, u32[]{:S(2)}, u32[]{:S(2)}) async-start(f32[64,4,8,128]{3,2,1,0:T(8,128)} %bitcast.1), calls=%async_computation | async-start | bytes 2097152 | tf_op jit(solution)/shard_map/all_to_all | solution.py:536
  18.7 0.7 copy-done.7
  19.4 0.1 fusion.68
  19.5 0.1 fusion.53
  19.7 0.1 broadcast_multiply_fusion.3
  19.7 0.1 broadcast_multiply_fusion.1
  19.8 0.7 copy-done.8
  20.5 0.0 copy-done.9
  20.5 1.1 %fusion.symbol_ref = f32[2,4,128,256]{3,2,1,0:T(8,128)S(1)} fusion(f32[2,1,128,16]{2,3,1,0:T(8,128)S(1)} %get-tuple-element.14, f32[2,1,128,16]{2,3,1,0:T(8,128)S(1)} %get-tuple-element.13, f32[2,1,128,16]{2,3,1,0:T(8,128)S(1)} %get-tuple-element.10, f32[2,1,128,16]{2,3,1,0:T(8,128)S(1)} %get-tuple-element.9, f32[16]{0:T(128)S(1)} %copy-done.8, ...), kind=kOutput, calls=%fused_computation | convolution fusion | flops 50511872 | bytes 1116416 | tf_op jit(solution)/shard_map/dot_general | solution.py:425
  21.6 25.2 %all-to-all-done.r_ref = f32[64,4,8,128]{3,2,1,0:T(8,128)S(1)} async-done(((f32[64,4,8,128]{3,2,1,0:T(8,128)}), f32[64,4,8,128]{3,2,1,0:T(8,128)S(1)}, u32[]{:S(2)}, u32[]{:S(2)}) %all-to-all-start) | async-done | bytes 1048608 | tf_op jit(solution)/shard_map/all_to_all | solution.py:536
  46.8 0.4 shard_map.111
  47.2 3.2 %collective-permute-start = (f32[320,128]{1,0:T(8,128)S(1)}, f32[320,128]{1,0:T(8,128)S(1)}, u32[]{:S(2)}, u32[]{:S(2)}) collective-permute-start(f32[320,128]{1,0:T(8,128)S(1)} %get-tuple-element.7), channel_id=1, source_target_pairs={{0,64},{64,0},{128,192},{192,128},{256,320},{320,256},{384,448},{4... | collective-permute-start | bytes 491528 | tf_op jit(solution)/shard_map/ppermute | solution.py:552
  50.4 4.9 %collective-permute-start.1 = (f32[320,128]{1,0:T(8,128)S(1)}, f32[320,128]{1,0:T(8,128)S(1)}, u32[]{:S(2)}, u32[]{:S(2)}) collective-permute-start(f32[320,128]{1,0:T(8,128)S(1)} %get-tuple-element.8), channel_id=1, source_target_pairs={{64,128},{128,64},{192,256},{256,192},{320,384},{384,320},{448,0},... | collective-permute-start | bytes 491528 | tf_op jit(solution)/shard_map/ppermute | solution.py:553
  55.3 0.1 fusion.65
  55.4 0.1 mul.283.damp_ref
  55.4 0.9 copy-done.6
  56.4 2.6 %shard_map.110.partial_ref = f32[64,4,8,128]{3,2,1,0:T(8,128)S(1)} custom-call(f32[4]{0:T(128)S(1)} %mul.283.damp_ref, f32[64,4,8,128]{3,2,1,0:T(8,128)S(1)} %all-to-all-done.r_ref, bf16[256,512]{1,0:T(8,128)(2,1)S(1)} %copy-done.5, f32[2,4,128,256]{3,2,1,0:T(8,128)S(1)} %fusion.symbol_ref, bf16[256,768]{1,0:T(8,128)(2,1)S(1)} %copy-done.4, ...), custom_call_target="tpu_custom_call" | custom-call | flops 1342177280 | bytes 6029344 | tf_op jit(solution)/shard_map/pallas_call | solution.py:374
  59.0 2.1 %shard_map.112 = f32[64,4,8,128]{3,2,1,0:T(8,128)} custom-call(s32[1]{0:T(128)} %bitcast.odd_ref, f32[64,4,8,128]{3,2,1,0:T(8,128)S(1)} %shard_map.110.partial_ref, f32[320,128]{1,0:T(8,128)S(1)} %collective-permute-done.first_ref, f32[320,128]{1,0:T(8,128)S(1)} %collective-permute-done.1.second_ref), custom_call_target="tpu_custom_call" | custom-call | flops 10485760 | bytes 2752520 | tf_op jit(solution)/shard_map/pallas_call | solution.py:374
  61.1 7.0 %all-to-all-start.1 = ((f32[64,4,8,128]{3,2,1,0:T(8,128)}), f32[64,4,8,128]{3,2,1,0:T(8,128)S(1)}, u32[]{:S(2)}, u32[]{:S(2)}) async-start(f32[64,4,8,128]{3,2,1,0:T(8,128)} %shard_map.112), calls=%async_computation.1 | async-start | bytes 2097152 | tf_op jit(solution)/shard_map/all_to_all | solution.py:556
  68.1 1.0 shard_map.113.local_ref
  69.1 27.2 %all-to-all-done.1 = f32[64,4,8,128]{3,2,1,0:T(8,128)S(1)} async-done(((f32[64,4,8,128]{3,2,1,0:T(8,128)}), f32[64,4,8,128]{3,2,1,0:T(8,128)S(1)}, u32[]{:S(2)}, u32[]{:S(2)}) %all-to-all-start.1) | async-done | bytes 1048608 | tf_op jit(solution)/shard_map/all_to_all | solution.py:556
  96.3 0.9 copy-done.2
  97.2 1.6 %shard_map.114 = f32[8,256,128]{2,1,0:T(8,128)} custom-call(f32[2048,128]{1,0:T(8,128)S(1)} %bitcast.14, f32[8,256,128]{2,1,0:T(8,128)S(1)} %shard_map.113.local_ref, bf16[256,512]{1,0:T(8,128)(2,1)S(1)} %copy-done.2), custom_call_target="tpu_custom_call" | custom-call | flops 402653184 | bytes 4718592 | tf_op jit(solution)/shard_map/pallas_call | solution.py:374
  (22 shorter events, 0.1 us)
Async XLA Ops:
  3.8 43.0 %all-to-all-start = ((f32[64,4,8,128]{3,2,1,0:T(8,128)}), f32[64,4,8,128]{3,2,1,0:T(8,128)S(1)}, u32[]{:S(2)}, u32[]{:S(2)}) async-start(f32[64,4,8,128]{3,2,1,0:T(8,128)} %bitcast.1), calls=%async_computation | async-start | bytes 2097152 | tf_op jit(solution)/shard_map/all_to_all | solution.py:536
  18.7 0.7 copy-start.7
  19.8 0.7 copy-start.8
  19.8 0.7 copy-start.9
  46.8 8.6 %copy-start.4 = (bf16[256,768]{1,0:T(8,128)(2,1)S(1)}, bf16[256,768]{1,0:T(8,128)(2,1)}, u32[]{:S(2)}) copy-start(bf16[256,768]{1,0:T(8,128)(2,1)} %constant.148.clone.inverse_ref) | copy-start | bytes 1179652
  46.8 8.6 %copy-start.5 = (bf16[256,512]{1,0:T(8,128)(2,1)S(1)}, bf16[256,512]{1,0:T(8,128)(2,1)}, u32[]{:S(2)}) copy-start(bf16[256,512]{1,0:T(8,128)(2,1)} %constant.147.clone.forward_ref) | copy-start | bytes 786436
  47.2 11.8 %collective-permute-start = (f32[320,128]{1,0:T(8,128)S(1)}, f32[320,128]{1,0:T(8,128)S(1)}, u32[]{:S(2)}, u32[]{:S(2)}) collective-permute-start(f32[320,128]{1,0:T(8,128)S(1)} %get-tuple-element.7), channel_id=1, source_target_pairs={{0,64},{64,0},{128,192},{192,128},{256,320},{320,256},{384,448},{4... | collective-permute-start | bytes 491528 | tf_op jit(solution)/shard_map/ppermute | solution.py:552
  50.4 8.6 %collective-permute-start.1 = (f32[320,128]{1,0:T(8,128)S(1)}, f32[320,128]{1,0:T(8,128)S(1)}, u32[]{:S(2)}, u32[]{:S(2)}) collective-permute-start(f32[320,128]{1,0:T(8,128)S(1)} %get-tuple-element.8), channel_id=1, source_target_pairs={{64,128},{128,64},{192,256},{256,192},{320,384},{384,320},{448,0},... | collective-permute-start | bytes 491528 | tf_op jit(solution)/shard_map/ppermute | solution.py:553
  55.4 1.0 copy-start.6
  61.1 7.0 %copy-start = (f32[8,256,128]{2,1,0:T(8,128)S(1)}, f32[8,256,128]{2,1,0:T(8,128)}, u32[]{:S(2)}) copy-start(f32[8,256,128]{2,1,0:T(8,128)} %u_ref.3) | copy-start | bytes 3145732
  61.1 7.0 %copy-start.1 = (bf16[256,512]{1,0:T(8,128)(2,1)S(1)}, bf16[256,512]{1,0:T(8,128)(2,1)}, u32[]{:S(2)}) copy-start(bf16[256,512]{1,0:T(8,128)(2,1)} %constant.149.clone.friction_ref) | copy-start | bytes 786436
  61.1 7.0 %copy-start.3 = (bf16[2,256,128]{2,1,0:T(8,128)(2,1)S(1)}, bf16[2,256,128]{2,1,0:T(8,128)(2,1)}, u32[]{:S(2)}) copy-start(bf16[2,256,128]{2,1,0:T(8,128)(2,1)} %constant.151.clone.shift_ref) | copy-start | bytes 393220
  61.1 35.1 %all-to-all-start.1 = ((f32[64,4,8,128]{3,2,1,0:T(8,128)}), f32[64,4,8,128]{3,2,1,0:T(8,128)S(1)}, u32[]{:S(2)}, u32[]{:S(2)}) async-start(f32[64,4,8,128]{3,2,1,0:T(8,128)} %shard_map.112), calls=%async_computation.1 | async-start | bytes 2097152 | tf_op jit(solution)/shard_map/all_to_all | solution.py:556
  96.3 1.0 copy-start.2

commit v3 on v2

--- a/solution.py
+++ b/solution.py
@@ -21,6 +21,7 @@
 HIGHEST_PRECISION = lax.Precision.HIGHEST
 FORWARD_STEPS = 4
 BACKWARD_STEPS = 2
+LOCAL_STEPS = 2
 
 
 def wide(table):
@@ -86,9 +87,7 @@
     result["inverse_second"] = jnp.asarray(wide(interleaved(inverse.T).T))
     result["forward_first"] = jnp.asarray(wide(forward))
     friction = friction_matrix().astype(ml_dtypes.bfloat16)
-    result["inverse_first"] = jnp.asarray(
-        np.concatenate([wide(inverse), friction], axis=1)
-    )
+    result["inverse_first"] = jnp.asarray(wide(inverse))
     result["friction"] = jnp.asarray(np.concatenate([friction, friction], axis=1))
     rows = 2 * rows_dev
     result["row_inner"] = bf16_table(
@@ -128,17 +127,31 @@
     return (2 * index - (POINTS - 1)).astype(F32) * (1.0 / (60 * POINTS))
 
 
-def forward_kernel(u_ref, table_ref, out_ref):
+def forward_kernel(u_hbm, table_hbm, out_ref, u_ref, table_ref, sems):
     planes, _, cells = u_ref.shape
-    first = pl.program_id(0) * planes
-    parts = [split(u_ref[k]) for k in range(planes)]
-    high, low = (jnp.concatenate(values, axis=1) for values in zip(*parts))
-    result = wide_dot(table_ref[...], high, low)
-    stride = out_ref.shape[0] // POINTS
-    for k in range(planes):
-        out_ref[pl.ds(first + k, POINTS, stride=stride), :] = result[
-            :, k * cells : (k + 1) * cells
-        ]
+    step = planes // FORWARD_STEPS
+    table_copy = pltpu.make_async_copy(table_hbm, table_ref, sems.at[FORWARD_STEPS])
+    copies = [
+        pltpu.make_async_copy(
+            u_hbm.at[pl.ds(i * step, step)], u_ref.at[pl.ds(i * step, step)], sems.at[i]
+        )
+        for i in range(FORWARD_STEPS)
+    ]
+    copies[0].start()
+    table_copy.start()
+    for copy in copies[1:]:
+        copy.start()
+    for i, copy in enumerate(copies):
+        copy.wait()
+        if i == 0:
+            table_copy.wait()
+        parts = [split(u_ref[k]) for k in range(i * step, (i + 1) * step)]
+        high, low = (jnp.concatenate(values, axis=1) for values in zip(*parts))
+        result = wide_dot(table_ref[...], high, low)
+        for k in range(step):
+            out_ref[pl.ds(i * step + k, POINTS, stride=planes), :] = result[
+                :, k * cells : (k + 1) * cells
+            ]
 
 
 def backward_kernel(w_ref, local_ref, table_ref, out_ref):
@@ -156,6 +169,7 @@
 
 def local_kernel(u_ref, friction_ref, shift_ref, out_ref):
     planes, _, cells = u_ref.shape
+    first = pl.program_id(0) * planes
     for k in range(planes):
         high, low = split(u_ref[k])
         friction = dot(friction_ref[...], jnp.concatenate([high, low], axis=0))
@@ -163,7 +177,7 @@
         for side in range(2):
             part = slice(side * HALF, (side + 1) * HALF)
             moved = dot(both[part], shift_ref[side])
-            out_ref[k, part, :] = friction[part] - moved * speed_over_60(
+            out_ref[first + k, part, :] = friction[part] - moved * speed_over_60(
                 side * HALF, HALF, cells
             )
 
@@ -227,7 +241,21 @@
             x_ref[POINTS : 2 * POINTS, at : at + cells] = low
 
 
-def middle_kernel(damp_ref, r_ref, forward_ref, symbol_ref, inverse_ref, inner_ref, out_ref, x_ref, y_ref):
+def first_friction(value):
+    index = lax.broadcasted_iota(jnp.int32, value.shape, 0)
+    weighted = value * (
+        (2 * index - (POINTS - 1)).astype(F32) * (FRICTION / POINTS)
+    )
+    later = jnp.where(index < POINTS - 1, pltpu.roll(weighted, POINTS - 1, 0), 0.0)
+    earlier = jnp.where(index > 0, pltpu.roll(weighted, 1, 0), 0.0)
+    return later - earlier
+
+
+def middle_kernel(
+    damp_ref, r_ref, forward_ref, symbol_ref, inverse_ref, inner_hbm, out_ref, x_ref, y_ref, inner_ref, sem
+):
+    inner_copy = pltpu.make_async_copy(inner_hbm, inner_ref, sem)
+    inner_copy.start()
     load_columns(r_ref, x_ref)
     spectrum = wide_dot(forward_ref[...], x_ref[0:POINTS, :], x_ref[POINTS:, :])
     width = spectrum.shape[1] // 4
@@ -262,36 +290,43 @@
             y_ref[POINTS + half * HALF : POINTS + (half + 1) * HALF, at : at + width] = low
     cells = width // 2
     owners = out_ref.shape[0] // 2
-    inverse = inverse_ref[...]
-    friction = inverse[:, 2 * POINTS :]
-    result = (
-        wide_dot(inverse, y_ref[0:POINTS, :], y_ref[POINTS:, :])
-        + dot(friction, x_ref[0:POINTS, :])
-        + dot(friction, x_ref[POINTS:, :])
-    )
-    for side in range(2):
-        part = slice(side * HALF, (side + 1) * HALF)
-        low_part = slice(POINTS + side * HALF, POINTS + (side + 1) * HALF)
-        moved = sum(
+    result = wide_dot(inverse_ref[...], y_ref[0:POINTS, :], y_ref[POINTS:, :])
+    inner_copy.wait()
+    moved = [
+        sum(
             dot(
                 jnp.concatenate(
-                    [x_ref[rows, q * width : (q + 1) * width] for q in range(4)], axis=0
+                    [
+                        x_ref[
+                            half + side * HALF : half + (side + 1) * HALF,
+                            q * width : (q + 1) * width,
+                        ]
+                        for q in range(4)
+                    ],
+                    axis=0,
                 ),
                 inner_ref[side],
             )
-            for rows in (part, low_part)
+            for half in (0, POINTS)
         )
-        speed = speed_over_60(side * HALF, HALF, width)
-        rows = owners // 2
-        for q in range(4):
-            value = (
-                result[part, q * width : (q + 1) * width]
-                - moved[q * HALF : (q + 1) * HALF] * speed
-            )
-            for band in range(2):
-                out_ref[
-                    band * owners + side * rows : band * owners + (side + 1) * rows, q
-                ] = value[:, band * cells : (band + 1) * cells].reshape(rows, -1, cells)
+        for side in range(2)
+    ]
+    rows = owners // 2
+    for q in range(4):
+        for band in range(2):
+            here = r_ref[band * owners : (band + 1) * owners, q].reshape(POINTS, cells)
+            friction = first_friction(here)
+            inside = slice(band * cells, (band + 1) * cells)
+            for side in range(2):
+                part = slice(side * HALF, (side + 1) * HALF)
+                value = (
+                    result[part, q * width : (q + 1) * width][:, inside]
+                    + friction[part]
+                    - moved[side][q * HALF : (q + 1) * HALF, inside]
+                    * speed_over_60(side * HALF, HALF, cells)
+                )
+                at = band * owners + side * rows
+                out_ref[at : at + rows, q] = value.reshape(rows, -1, cells)
 
 
 def lane_weight(lane, first_row, last_row, weight):
@@ -300,15 +335,14 @@
 
 def edge_kernel(odd_ref, partial_ref, first_ref, second_ref, out_ref):
     for step in range(4):
-        pl.when(pl.program_id(0) == step)(
-            lambda step=step: edge_part(
-                step // 2, step % 2, odd_ref, partial_ref, first_ref, second_ref, out_ref
-            )
+        edge_part(
+            step // 2, step % 2, odd_ref, partial_ref, first_ref, second_ref, out_ref
         )
 
 
 def edge_part(band, side, odd_ref, partial_ref, first_ref, second_ref, out_ref):
-    owners, _, _, cells = out_ref.shape
+    members, _, _, cells = out_ref.shape
+    owners = members // 4
     band_rows = cells // NY
     stencil = dict((PLUS, MINUS)[side])
     weights = [stencil.get(s if band else -s) for s in (1, 2, 3)]
@@ -340,7 +374,7 @@
                 [turn(thin, NY * (row - q - 4 * h)) for h in range(2)], axis=0
             )
             moved += lane_weight(lane, row, row + 1, weights[2]) * third
-        out_ref[:, q] = partial_ref[block, q] - (moved * speed).reshape(owners, -1, cells)
+        out_ref[block, q] = partial_ref[block, q] - (moved * speed).reshape(owners, -1, cells)
 
 
 VMEM_SPEC = pl.BlockSpec(memory_space=pltpu.VMEM)
@@ -441,25 +475,32 @@
         forward_kernel,
         [((points * planes, cells), F32)],
         (off_chip(density), off_chip(table["forward_second"])),
+        (
+            pltpu.VMEM(density.shape, F32),
+            pltpu.VMEM((points, 2 * points), BF16),
+            pltpu.SemaphoreType.DMA((FORWARD_STEPS + 1,)),
+        ),
         flops=6 * points * points * planes * cells,
         keep=False,
-        grid=(FORWARD_STEPS,),
-        in_specs=[
-            pl.BlockSpec((planes // FORWARD_STEPS, points, cells), lambda i: (i, 0, 0)),
-            pl.BlockSpec((points, 2 * points), lambda i: (0, 0)),
-        ],
-        out_specs=[pl.BlockSpec((points * planes, cells), lambda i: (0, 0))],
+        in_specs=[pl.BlockSpec(memory_space=pl.ANY)] * 2,
     )
     return sent.reshape(points // 4, 4, planes, cells)
 
 
 def stage_local(density, table):
     planes, points, cells = density.shape
+    friction, shift = table["friction"], table["column_shift"]
     return call(
         local_kernel,
         [((planes, points, cells), F32)],
-        (density, table["friction"], table["column_shift"]),
+        (off_chip(density), off_chip(friction), off_chip(shift)),
         flops=6 * points * points * planes * cells,
+        grid=(LOCAL_STEPS,),
+        in_specs=[
+            pl.BlockSpec((planes // LOCAL_STEPS, points, cells), lambda i: (i, 0, 0)),
+            pl.BlockSpec(friction.shape, lambda i: (0, 0)),
+            pl.BlockSpec(shift.shape, lambda i: (0, 0, 0)),
+        ],
     )
 
 
@@ -473,35 +514,33 @@
 def stage_middle(damp, columns, symbol, table):
     _, _, _, cells = columns.shape
     width = 8 * cells
+    inner = table["row_inner"]
     scratch = pltpu.VMEM((2 * POINTS, width), BF16)
     return call(
         middle_kernel,
         [(columns.shape, F32)],
         (
             damp,
-            columns,
-            table["forward_first"],
-            symbol,
-            table["inverse_first"],
-            table["row_inner"],
+            on_chip(columns),
+            on_chip(table["forward_first"]),
+            on_chip(symbol),
+            on_chip(table["inverse_first"]),
+            off_chip(inner),
         ),
-        (scratch, scratch),
+        (scratch, scratch, pltpu.VMEM(inner.shape, BF16), pltpu.SemaphoreType.DMA),
         20 * POINTS * POINTS * width,
-        smem=1,
+        in_specs=[SMEM_SPEC] + [VMEM_SPEC] * 4 + [pl.BlockSpec(memory_space=pl.ANY)],
     )
 
 
 def stage_edge(odd, partial, first, second):
-    members, _, planes, cells = partial.shape
     return call(
         edge_kernel,
         [(partial.shape, F32)],
-        (odd, on_chip(partial), on_chip(first), on_chip(second)),
+        (odd, partial, first, second),
         flops=40 * partial.size,
+        smem=1,
         keep=False,
-        grid=(4,),
-        in_specs=[SMEM_SPEC] + [VMEM_SPEC] * 3,
-        out_specs=[pl.BlockSpec((members // 4, 4, planes, cells), lambda i: (i, 0, 0, 0))],
     )
 
 

time: 99.3 us -> 97.4 us (0.981)
  local copies, waits for them, and re-layouts: 3.35 us -> 1.44 us
  Pallas kernels: 11.5 us -> 12.9 us
  waiting for transfers between devices: 52.4 us -> 51 us
    unnamed x20 -> x12, local copies, waits for them, and re-layouts: 3.26 us -> 1.35 us
    pallas_call x6, Pallas kernels: 11.5 us -> 12.9 us  [call(): pl.pallas_call(kernel, grid=grid, out_shape=shapes[0] if single else shap...]
    all_to_all x1, waiting for transfers between devices: 27.2 us -> 25.8 us  [local(): lax.all_to_all(back, group, split_axis=0, concat_axis=0, tiled=True)]
  transfers between devices with their start and end apart: 4 -> 4, of which waited for: 2 -> 2; matrix products, arithmetic and copies ran while one was open for 2% -> 2% of each run, Pallas kernels for 4% -> 6%
where the time goes in v3:
time: 97.4 us; the launch traced here: 97 us
  waiting for transfers between devices  51 us (52%)
  starting transfers between devices  29.9 us (31%)
  Pallas kernels  12.9 us (13%)
  local copies, waits for them, and re-layouts  1.44 us (1%)
  matrix products  1.12 us (1%)
    all_to_all x1, waiting for transfers between devices, local(): lax.all_to_all(back, group, split_axis=0, concat_axis=0, tiled=True)  25.8 us
    all_to_all x1, waiting for transfers between devices, local(): lax.all_to_all(sent, group, split_axis=0, concat_axis=0, tiled=True)  25.2 us
    all_to_all x1, starting transfers between devices, local(): lax.all_to_all(sent, group, split_axis=0, concat_axis=0, tiled=True)  14.8 us
    pallas_call x6, Pallas kernels, call(): pl.pallas_call(kernel, grid=grid, out_shape=shapes[0] if single else shap...  12.9 us
    all_to_all x1, starting transfers between devices, local(): lax.all_to_all(back, group, split_axis=0, concat_axis=0, tiled=True)  6.96 us
    ppermute x1, starting transfers between devices, local(): second = lax.ppermute(second, 'y', swaps[1])  4.87 us
    ppermute x1, starting transfers between devices, local(): first = lax.ppermute(first, 'y', swaps[0])  3.2 us
  transfers between devices with their start and end apart: 4, of which 2 were waited for; matrix products, arithmetic and copies ran while one was open for 2% of the time, Pallas kernels for 6%

profile of v3, /device:TPU:1, one launch (start us, length us, event | category | flops | bytes accessed | tf_op | source)
XLA Modules:
  0.0 97.0 jit_solution(9943851174704514946)
XLA Ops:
  0.0 3.5 %shard_map.109 = f32[2048,128]{1,0:T(8,128)} custom-call(f32[8,256,128]{2,1,0:T(8,128)} %u_ref.1, bf16[256,512]{1,0:T(8,128)(2,1)} %constant.145.clone.table_hbm), custom_call_target="tpu_custom_call" | custom-call | flops 402653184 | bytes 2621440 | tf_op jit(solution)/shard_map/pallas_call | solution.py:408
  3.5 14.8 %all-to-all-start = ((f32[64,4,8,128]{3,2,1,0:T(8,128)}), f32[64,4,8,128]{3,2,1,0:T(8,128)S(1)}, u32[]{:S(2)}, u32[]{:S(2)}) async-start(f32[64,4,8,128]{3,2,1,0:T(8,128)} %bitcast.1), calls=%async_computation | async-start | bytes 2097152 | tf_op jit(solution)/shard_map/all_to_all | solution.py:575
  18.4 0.0 copy-start.3
  18.4 0.7 copy-done.3
  19.1 0.1 fusion.68
  19.2 0.1 fusion.53
  19.3 0.1 broadcast_multiply_fusion.3
  19.4 0.1 broadcast_multiply_fusion.1
  19.5 0.7 copy-done.4
  20.2 0.0 copy-done.5
  20.2 1.1 %fusion.symbol_ref = f32[2,4,128,256]{3,2,1,0:T(8,128)S(1)} fusion(f32[2,1,128,16]{2,3,1,0:T(8,128)S(1)} %get-tuple-element.14, f32[2,1,128,16]{2,3,1,0:T(8,128)S(1)} %get-tuple-element.13, f32[2,1,128,16]{2,3,1,0:T(8,128)S(1)} %get-tuple-element.10, f32[2,1,128,16]{2,3,1,0:T(8,128)S(1)} %get-tuple-element.9, f32[16]{0:T(128)S(1)} %copy-done.4, ...), kind=kOutput, calls=%fused_computation | convolution fusion | flops 50511872 | bytes 1116416 | tf_op jit(solution)/shard_map/dot_general | solution.py:459
  21.3 25.2 %all-to-all-done.r_ref = f32[64,4,8,128]{3,2,1,0:T(8,128)S(1)} async-done(((f32[64,4,8,128]{3,2,1,0:T(8,128)}), f32[64,4,8,128]{3,2,1,0:T(8,128)S(1)}, u32[]{:S(2)}, u32[]{:S(2)}) %all-to-all-start) | async-done | bytes 1048608 | tf_op jit(solution)/shard_map/all_to_all | solution.py:575
  46.5 0.4 shard_map.111
  46.9 3.2 %collective-permute-start = (f32[320,128]{1,0:T(8,128)S(1)}, f32[320,128]{1,0:T(8,128)S(1)}, u32[]{:S(2)}, u32[]{:S(2)}) collective-permute-start(f32[320,128]{1,0:T(8,128)S(1)} %get-tuple-element.7), channel_id=1, source_target_pairs={{0,64},{64,0},{128,192},{192,128},{256,320},{320,256},{384,448},{4... | collective-permute-start | bytes 491528 | tf_op jit(solution)/shard_map/ppermute | solution.py:591
  50.1 4.9 %collective-permute-start.1 = (f32[320,128]{1,0:T(8,128)S(1)}, f32[320,128]{1,0:T(8,128)S(1)}, u32[]{:S(2)}, u32[]{:S(2)}) collective-permute-start(f32[320,128]{1,0:T(8,128)S(1)} %get-tuple-element.8), channel_id=1, source_target_pairs={{64,128},{128,64},{192,256},{256,192},{320,384},{384,320},{448,0},... | collective-permute-start | bytes 491528 | tf_op jit(solution)/shard_map/ppermute | solution.py:592
  55.0 0.1 fusion.65
  55.0 0.1 mul.283.damp_ref
  55.1 3.4 %shard_map.110.partial_ref = f32[64,4,8,128]{3,2,1,0:T(8,128)S(1)} custom-call(f32[4]{0:T(128)S(1)} %mul.283.damp_ref, f32[64,4,8,128]{3,2,1,0:T(8,128)S(1)} %all-to-all-done.r_ref, bf16[256,512]{1,0:T(8,128)(2,1)S(1)} %copy-done.1, f32[2,4,128,256]{3,2,1,0:T(8,128)S(1)} %fusion.symbol_ref, bf16[256,512]{1,0:T(8,128)(2,1)S(1)} %copy-done.2, ...), custom_call_target="tpu_custom_call" | custom-call | flops 1342177280 | bytes 5767200 | tf_op jit(solution)/shard_map/pallas_call | solution.py:408
  58.5 1.7 %shard_map.112 = f32[64,4,8,128]{3,2,1,0:T(8,128)} custom-call(s32[1]{0:T(128)} %bitcast.odd_ref, f32[64,4,8,128]{3,2,1,0:T(8,128)S(1)} %shard_map.110.partial_ref, f32[320,128]{1,0:T(8,128)S(1)} %collective-permute-done.first_ref, f32[320,128]{1,0:T(8,128)S(1)} %collective-permute-done.1.second_ref), custom_call_target="tpu_custom_call" | custom-call | flops 10485760 | bytes 2752520 | tf_op jit(solution)/shard_map/pallas_call | solution.py:408
  60.2 7.0 %all-to-all-start.1 = ((f32[64,4,8,128]{3,2,1,0:T(8,128)}), f32[64,4,8,128]{3,2,1,0:T(8,128)S(1)}, u32[]{:S(2)}, u32[]{:S(2)}) async-start(f32[64,4,8,128]{3,2,1,0:T(8,128)} %shard_map.112), calls=%async_computation.1 | async-start | bytes 2097152 | tf_op jit(solution)/shard_map/all_to_all | solution.py:595
  67.1 0.0 copy-start
  67.2 2.4 %shard_map.113.local_ref = f32[8,256,128]{2,1,0:T(8,128)S(1)} custom-call(f32[8,256,128]{2,1,0:T(8,128)} %u_ref.1, bf16[256,512]{1,0:T(8,128)(2,1)} %constant.149.clone.friction_ref, bf16[2,256,128]{2,1,0:T(8,128)(2,1)} %constant.151.clone.shift_ref), custom_call_target="tpu_custom_call" | custom-call | flops 402653184 | bytes 2883584 | tf_op jit(solution)/shard_map/pallas_call | solution.py:408
  69.5 25.8 %all-to-all-done.1 = f32[64,4,8,128]{3,2,1,0:T(8,128)S(1)} async-done(((f32[64,4,8,128]{3,2,1,0:T(8,128)}), f32[64,4,8,128]{3,2,1,0:T(8,128)S(1)}, u32[]{:S(2)}, u32[]{:S(2)}) %all-to-all-start.1) | async-done | bytes 1048608 | tf_op jit(solution)/shard_map/all_to_all | solution.py:595
  95.3 1.7 %shard_map.114 = f32[8,256,128]{2,1,0:T(8,128)} custom-call(f32[2048,128]{1,0:T(8,128)S(1)} %bitcast.14, f32[8,256,128]{2,1,0:T(8,128)S(1)} %shard_map.113.local_ref, bf16[256,512]{1,0:T(8,128)(2,1)S(1)} %copy-done), custom_call_target="tpu_custom_call" | custom-call | flops 402653184 | bytes 4718592 | tf_op jit(solution)/shard_map/pallas_call | solution.py:408
  (14 shorter events, 0.0 us)
Async XLA Ops:
  3.5 43.0 %all-to-all-start = ((f32[64,4,8,128]{3,2,1,0:T(8,128)}), f32[64,4,8,128]{3,2,1,0:T(8,128)S(1)}, u32[]{:S(2)}, u32[]{:S(2)}) async-start(f32[64,4,8,128]{3,2,1,0:T(8,128)} %bitcast.1), calls=%async_computation | async-start | bytes 2097152 | tf_op jit(solution)/shard_map/all_to_all | solution.py:575
  18.4 0.7 copy-start.3
  19.5 0.7 copy-start.4
  19.5 0.7 copy-start.5
  46.5 8.6 %copy-start.1 = (bf16[256,512]{1,0:T(8,128)(2,1)S(1)}, bf16[256,512]{1,0:T(8,128)(2,1)}, u32[]{:S(2)}) copy-start(bf16[256,512]{1,0:T(8,128)(2,1)} %constant.147.clone.forward_ref) | copy-start | bytes 786436
  46.5 8.6 %copy-start.2 = (bf16[256,512]{1,0:T(8,128)(2,1)S(1)}, bf16[256,512]{1,0:T(8,128)(2,1)}, u32[]{:S(2)}) copy-start(bf16[256,512]{1,0:T(8,128)(2,1)} %constant.148.clone.inverse_ref) | copy-start | bytes 786436
  46.9 11.6 %collective-permute-start = (f32[320,128]{1,0:T(8,128)S(1)}, f32[320,128]{1,0:T(8,128)S(1)}, u32[]{:S(2)}, u32[]{:S(2)}) collective-permute-start(f32[320,128]{1,0:T(8,128)S(1)} %get-tuple-element.7), channel_id=1, source_target_pairs={{0,64},{64,0},{128,192},{192,128},{256,320},{320,256},{384,448},{4... | collective-permute-start | bytes 491528 | tf_op jit(solution)/shard_map/ppermute | solution.py:591
  50.1 8.4 %collective-permute-start.1 = (f32[320,128]{1,0:T(8,128)S(1)}, f32[320,128]{1,0:T(8,128)S(1)}, u32[]{:S(2)}, u32[]{:S(2)}) collective-permute-start(f32[320,128]{1,0:T(8,128)S(1)} %get-tuple-element.8), channel_id=1, source_target_pairs={{64,128},{128,64},{192,256},{256,192},{320,384},{384,320},{448,0},... | collective-permute-start | bytes 491528 | tf_op jit(solution)/shard_map/ppermute | solution.py:592
  60.2 35.1 %all-to-all-start.1 = ((f32[64,4,8,128]{3,2,1,0:T(8,128)}), f32[64,4,8,128]{3,2,1,0:T(8,128)S(1)}, u32[]{:S(2)}, u32[]{:S(2)}) async-start(f32[64,4,8,128]{3,2,1,0:T(8,128)} %shard_map.112), calls=%async_computation.1 | async-start | bytes 2097152 | tf_op jit(solution)/shard_map/all_to_all | solution.py:595
  67.1 28.2 %copy-start = (bf16[256,512]{1,0:T(8,128)(2,1)S(1)}, bf16[256,512]{1,0:T(8,128)(2,1)}, u32[]{:S(2)}) copy-start(bf16[256,512]{1,0:T(8,128)(2,1)} %constant.146.clone.table_ref) | copy-start | bytes 786436

commit v4 on v3

--- a/solution.py
+++ b/solution.py
@@ -1,3 +1,4 @@
+import functools
 import math
 
 import jax
@@ -19,8 +20,8 @@
 F32 = jnp.float32
 BF16 = jnp.bfloat16
 HIGHEST_PRECISION = lax.Precision.HIGHEST
-FORWARD_STEPS = 4
-BACKWARD_STEPS = 2
+FORWARD_STEPS = 1
+BACKWARD_STEPS = 1
 LOCAL_STEPS = 2
 
 
@@ -252,10 +253,8 @@
 
 
 def middle_kernel(
-    damp_ref, r_ref, forward_ref, symbol_ref, inverse_ref, inner_hbm, out_ref, x_ref, y_ref, inner_ref, sem
+    damp_ref, r_ref, forward_ref, symbol_ref, inverse_ref, inner_ref, out_ref, x_ref, y_ref
 ):
-    inner_copy = pltpu.make_async_copy(inner_hbm, inner_ref, sem)
-    inner_copy.start()
     load_columns(r_ref, x_ref)
     spectrum = wide_dot(forward_ref[...], x_ref[0:POINTS, :], x_ref[POINTS:, :])
     width = spectrum.shape[1] // 4
@@ -291,7 +290,6 @@
     cells = width // 2
     owners = out_ref.shape[0] // 2
     result = wide_dot(inverse_ref[...], y_ref[0:POINTS, :], y_ref[POINTS:, :])
-    inner_copy.wait()
     moved = [
         sum(
             dot(
@@ -333,28 +331,27 @@
     return jnp.where((lane >= first_row * NY) & (lane < last_row * NY), weight, 0.0)
 
 
-def edge_kernel(odd_ref, partial_ref, first_ref, second_ref, out_ref):
-    for step in range(4):
-        edge_part(
-            step // 2, step % 2, odd_ref, partial_ref, first_ref, second_ref, out_ref
-        )
-
-
-def edge_part(band, side, odd_ref, partial_ref, first_ref, second_ref, out_ref):
+def edge_kernel(odd_band, odd_ref, partial_ref, halo_ref, *refs):
+    out_ref = refs[-1]
+    for odd in range(2):
+
+        @pl.when(odd_ref[0] == odd)
+        def _(band=odd_band if odd else 1 - odd_band):
+            for side in range(2):
+                edge_part(band, side, partial_ref, halo_ref, out_ref)
+
+
+def edge_part(band, side, partial_ref, halo_ref, out_ref):
     members, _, _, cells = out_ref.shape
-    owners = members // 4
+    owners = members // 2
     band_rows = cells // NY
     stencil = dict((PLUS, MINUS)[side])
     weights = [stencil.get(s if band else -s) for s in (1, 2, 3)]
-    odd = (odd_ref[0] == 1) != bool(band)
     lane = lax.broadcasted_iota(jnp.int32, (HALF, cells), 1)
-
-    def received(rows):
-        return jnp.where(odd, first_ref[rows, :], second_ref[rows, :])
-
-    pair = received(slice(side * HALF, (side + 1) * HALF))
-    thin = received(slice(POINTS, POINTS + HALF // 2)) if weights[2] else None
+    pair = halo_ref[side * HALF : (side + 1) * HALF, :]
+    thin = halo_ref[POINTS : POINTS + HALF // 2, :]
     speed = speed_over_60(side * HALF, HALF, cells)
+    here = slice(side * owners, (side + 1) * owners)
     block = slice((2 * band + side) * owners, (2 * band + side + 1) * owners)
     for q in range(4):
         moved = 0.0
@@ -368,13 +365,13 @@
                 near = s - 2
                 rows = (max(near, 0), s)
             moved += lane_weight(lane, *rows, weight) * turn(pair, NY * (near - 2 * q))
-        if thin is not None:
+        if weights[2] is not None:
             row = band_rows - 1 if band else 0
             third = jnp.concatenate(
                 [turn(thin, NY * (row - q - 4 * h)) for h in range(2)], axis=0
             )
             moved += lane_weight(lane, row, row + 1, weights[2]) * third
-        out_ref[block, q] = partial_ref[block, q] - (moved * speed).reshape(owners, -1, cells)
+        out_ref[here, q] = partial_ref[block, q] - (moved * speed).reshape(owners, -1, cells)
 
 
 VMEM_SPEC = pl.BlockSpec(memory_space=pltpu.VMEM)
@@ -514,34 +511,47 @@
 def stage_middle(damp, columns, symbol, table):
     _, _, _, cells = columns.shape
     width = 8 * cells
-    inner = table["row_inner"]
     scratch = pltpu.VMEM((2 * POINTS, width), BF16)
     return call(
         middle_kernel,
         [(columns.shape, F32)],
         (
             damp,
-            on_chip(columns),
-            on_chip(table["forward_first"]),
-            on_chip(symbol),
-            on_chip(table["inverse_first"]),
-            off_chip(inner),
+            columns,
+            table["forward_first"],
+            symbol,
+            table["inverse_first"],
+            table["row_inner"],
         ),
-        (scratch, scratch, pltpu.VMEM(inner.shape, BF16), pltpu.SemaphoreType.DMA),
+        (scratch, scratch),
         20 * POINTS * POINTS * width,
-        in_specs=[SMEM_SPEC] + [VMEM_SPEC] * 4 + [pl.BlockSpec(memory_space=pl.ANY)],
-    )
-
-
-def stage_edge(odd, partial, first, second):
-    return call(
-        edge_kernel,
-        [(partial.shape, F32)],
-        (odd, partial, first, second),
-        flops=40 * partial.size,
         smem=1,
-        keep=False,
-    )
+    )
+
+
+def stage_edge(odd, partial, halo, odd_band, back=None):
+    members, _, planes, cells = partial.shape
+
+    def place(_, odd_ref):
+        return (jnp.where(odd_ref[0] == 1, odd_band, 1 - odd_band), 0, 0, 0)
+
+    given = [] if back is None else [off_chip(back)]
+    return pl.pallas_call(
+        functools.partial(edge_kernel, odd_band),
+        out_shape=pltpu.HBM(partial.shape, F32),
+        grid_spec=pltpu.PrefetchScalarGridSpec(
+            num_scalar_prefetch=1,
+            grid=(1,),
+            in_specs=[VMEM_SPEC] * 2 + [pl.BlockSpec(memory_space=pl.ANY)] * len(given),
+            out_specs=pl.BlockSpec((members // 2, 4, planes, cells), place),
+        ),
+        input_output_aliases={3: 0} if given else {},
+        cost_estimate=pl.CostEstimate(
+            flops=20 * partial.size, bytes_accessed=4 * partial.size, transcendentals=0
+        ),
+        compiler_params=pltpu.CompilerParams(vmem_limit_bytes=24 << 20),
+        name="edge_second" if given else "edge_first",
+    )(odd, on_chip(partial), on_chip(halo), *given)
 
 
 def stage_backward(panels, here, table):
@@ -591,7 +601,8 @@
     first = lax.ppermute(first, "y", swaps[0])
     second = lax.ppermute(second, "y", swaps[1])
     partial = stage_middle(damp, columns, symbol, table)
-    back = stage_edge(odd, partial, first, second)
+    back = stage_edge(odd, partial, first, 0)
+    back = stage_edge(odd, partial, second, 1, back)
     panels = lax.all_to_all(back, group, split_axis=0, concat_axis=0, tiled=True)
     return stage_backward(panels, here, table)
 

time: 97.4 us -> 97.9 us (level)
  waiting for transfers between devices: 51 us -> 52.5 us
    pallas_call x6 -> x5, Pallas kernels: 12.9 us -> 9.71 us  [call(): pl.pallas_call(kernel, grid=grid, out_shape=shapes[0] if single else shap...]
    pallas_call x0 -> x2, Pallas kernels: none -> 2.34 us  [stage_edge(): pl.pallas_call(functools.partial(edge_kernel, odd_band), out_shape=pltpu....]
    ppermute x1, waiting for transfers between devices: 0.01 us -> 1.51 us  [local(): first = lax.ppermute(first, 'y', swaps[0])]
    ppermute x1, starting transfers between devices: 3.2 us -> 1.92 us  [local(): first = lax.ppermute(first, 'y', swaps[0])]
  transfers between devices with their start and end apart: 4 -> 4, of which waited for: 2 -> 3; matrix products, arithmetic and copies ran while one was open for 2% -> 2% of each run, Pallas kernels for 6% -> 6%
where the time goes in v4:
time: 97.9 us; the launch traced here: 97.5 us
  waiting for transfers between devices  52.5 us (54%)
  starting transfers between devices  29.7 us (30%)
  Pallas kernels  12 us (12%)
  local copies, waits for them, and re-layouts  1.44 us (1%)
  matrix products  1.12 us (1%)
    all_to_all x1, waiting for transfers between devices, local(): lax.all_to_all(back, group, split_axis=0, concat_axis=0, tiled=True)  25.8 us
    all_to_all x1, waiting for transfers between devices, local(): lax.all_to_all(sent, group, split_axis=0, concat_axis=0, tiled=True)  25.2 us
    all_to_all x1, starting transfers between devices, local(): lax.all_to_all(sent, group, split_axis=0, concat_axis=0, tiled=True)  14.8 us
    pallas_call x5, Pallas kernels, call(): pl.pallas_call(kernel, grid=grid, out_shape=shapes[0] if single else shap...  9.71 us
    all_to_all x1, starting transfers between devices, local(): lax.all_to_all(back, group, split_axis=0, concat_axis=0, tiled=True)  7.83 us
    ppermute x1, starting transfers between devices, local(): second = lax.ppermute(second, 'y', swaps[1])  5.1 us
    pallas_call x2, Pallas kernels, stage_edge(): pl.pallas_call(functools.partial(edge_kernel, odd_band), out_shape=pltpu....  2.34 us
  transfers between devices with their start and end apart: 4, of which 3 were waited for; matrix products, arithmetic and copies ran while one was open for 2% of the time, Pallas kernels for 6%

profile of v4, /device:TPU:1, one launch (start us, length us, event | category | flops | bytes accessed | tf_op | source)
XLA Modules:
  0.0 97.5 jit_solution(13600036001677478319)
XLA Ops:
  0.0 2.9 %shard_map.109 = f32[2048,128]{1,0:T(8,128)} custom-call(f32[8,256,128]{2,1,0:T(8,128)} %u_ref.1, bf16[256,512]{1,0:T(8,128)(2,1)} %constant.145.clone.table_hbm), custom_call_target="tpu_custom_call" | custom-call | flops 402653184 | bytes 2621440 | tf_op jit(solution)/shard_map/pallas_call | solution.py:405
  2.9 14.8 %all-to-all-start = ((f32[64,4,8,128]{3,2,1,0:T(8,128)}), f32[64,4,8,128]{3,2,1,0:T(8,128)S(1)}, u32[]{:S(2)}, u32[]{:S(2)}) async-start(f32[64,4,8,128]{3,2,1,0:T(8,128)} %bitcast.1), calls=%async_computation | async-start | bytes 2097152 | tf_op jit(solution)/shard_map/all_to_all | solution.py:585
  17.8 0.7 copy-done.4
  18.5 0.1 fusion.68
  18.6 0.1 fusion.53
  18.8 0.1 broadcast_multiply_fusion.3
  18.9 0.1 broadcast_multiply_fusion.1
  18.9 0.7 copy-done.5
  19.6 0.0 copy-done.6
  19.6 1.1 %fusion.symbol_ref = f32[2,4,128,256]{3,2,1,0:T(8,128)S(1)} fusion(f32[2,1,128,16]{2,3,1,0:T(8,128)S(1)} %get-tuple-element.14, f32[2,1,128,16]{2,3,1,0:T(8,128)S(1)} %get-tuple-element.13, f32[2,1,128,16]{2,3,1,0:T(8,128)S(1)} %get-tuple-element.10, f32[2,1,128,16]{2,3,1,0:T(8,128)S(1)} %get-tuple-element.9, f32[16]{0:T(128)S(1)} %copy-done.5, ...), kind=kOutput, calls=%fused_computation | convolution fusion | flops 50511872 | bytes 1116416 | tf_op jit(solution)/shard_map/dot_general | solution.py:456
  20.7 25.2 %all-to-all-done.r_ref = f32[64,4,8,128]{3,2,1,0:T(8,128)S(1)} async-done(((f32[64,4,8,128]{3,2,1,0:T(8,128)}), f32[64,4,8,128]{3,2,1,0:T(8,128)S(1)}, u32[]{:S(2)}, u32[]{:S(2)}) %all-to-all-start) | async-done | bytes 1048608 | tf_op jit(solution)/shard_map/all_to_all | solution.py:585
  45.9 0.4 shard_map.111
  46.3 5.1 %collective-permute-start = (f32[320,128]{1,0:T(8,128)S(1)}, f32[320,128]{1,0:T(8,128)S(1)}, u32[]{:S(2)}, u32[]{:S(2)}) collective-permute-start(f32[320,128]{1,0:T(8,128)S(1)} %get-tuple-element.7), channel_id=1, source_target_pairs={{64,128},{128,64},{192,256},{256,192},{320,384},{384,320},{448,0},... | collective-permute-start | bytes 491528 | tf_op jit(solution)/shard_map/ppermute | solution.py:602
  51.4 1.9 %collective-permute-start.1 = (f32[320,128]{1,0:T(8,128)S(1)}, f32[320,128]{1,0:T(8,128)S(1)}, u32[]{:S(2)}, u32[]{:S(2)}) collective-permute-start(f32[320,128]{1,0:T(8,128)S(1)} %get-tuple-element.8), channel_id=1, source_target_pairs={{0,64},{64,0},{128,192},{192,128},{256,320},{320,256},{384,448},{4... | collective-permute-start | bytes 491528 | tf_op jit(solution)/shard_map/ppermute | solution.py:601
  53.3 0.1 fusion.65
  53.4 0.1 mul.283.damp_ref
  53.5 2.4 %shard_map.110.partial_ref = f32[64,4,8,128]{3,2,1,0:T(8,128)S(1)} custom-call(f32[4]{0:T(128)S(1)} %mul.283.damp_ref, f32[64,4,8,128]{3,2,1,0:T(8,128)S(1)} %all-to-all-done.r_ref, bf16[256,512]{1,0:T(8,128)(2,1)S(1)} %copy-done.3, f32[2,4,128,256]{3,2,1,0:T(8,128)S(1)} %fusion.symbol_ref, bf16[256,512]{1,0:T(8,128)(2,1)S(1)} %copy-done.2, ...), custom_call_target="tpu_custom_call" | custom-call | flops 1342177280 | bytes 5767200 | tf_op jit(solution)/shard_map/pallas_call | solution.py:405
  56.0 1.5 %collective-permute-done.1.halo_ref = f32[320,128]{1,0:T(8,128)S(1)} collective-permute-done((f32[320,128]{1,0:T(8,128)S(1)}, f32[320,128]{1,0:T(8,128)S(1)}, u32[]{:S(2)}, u32[]{:S(2)}) %collective-permute-start.1) | collective-permute-done | bytes 163872 | tf_op jit(solution)/shard_map/ppermute | solution.py:601
  57.5 1.2 %edge_first.1.refs_0_ = f32[64,4,8,128]{3,2,1,0:T(8,128)} custom-call(s32[1]{0:T(128)} %bitcast.odd_ref, f32[64,4,8,128]{3,2,1,0:T(8,128)S(1)} %shard_map.110.partial_ref, f32[320,128]{1,0:T(8,128)S(1)} %collective-permute-done.1.halo_ref), custom_call_target="tpu_custom_call" | custom-call | flops 5242880 | bytes 1048576 | tf_op jit(solution)/shard_map/edge_first/pallas_call | solution.py:539
  58.7 1.2 %edge_second.1 = f32[64,4,8,128]{3,2,1,0:T(8,128)} custom-call(s32[1]{0:T(128)} %bitcast.odd_ref, f32[64,4,8,128]{3,2,1,0:T(8,128)S(1)} %shard_map.110.partial_ref, f32[320,128]{1,0:T(8,128)S(1)} %collective-permute-done.halo_ref, f32[64,4,8,128]{3,2,1,0:T(8,128)} %edge_first.1.refs_0_), custom_call_target="tpu_custom_call", output_to_operand_aliasing={{}: (3, {})} | custom-call | flops 5242880 | bytes 1048576 | tf_op jit(solution)/shard_map/edge_second/pallas_call | solution.py:539
  59.8 7.8 %all-to-all-start.1 = ((f32[64,4,8,128]{3,2,1,0:T(8,128)}), f32[64,4,8,128]{3,2,1,0:T(8,128)S(1)}, u32[]{:S(2)}, u32[]{:S(2)}) async-start(f32[64,4,8,128]{3,2,1,0:T(8,128)} %edge_second.1), calls=%async_computation.1 | async-start | bytes 2097152 | tf_op jit(solution)/shard_map/all_to_all | solution.py:606
  67.7 2.4 %shard_map.112.local_ref = f32[8,256,128]{2,1,0:T(8,128)S(1)} custom-call(f32[8,256,128]{2,1,0:T(8,128)} %u_ref.1, bf16[256,512]{1,0:T(8,128)(2,1)} %constant.149.clone.friction_ref, bf16[2,256,128]{2,1,0:T(8,128)(2,1)} %constant.151.clone.shift_ref), custom_call_target="tpu_custom_call" | custom-call | flops 402653184 | bytes 2883584 | tf_op jit(solution)/shard_map/pallas_call | solution.py:405
  70.0 25.8 %all-to-all-done.1 = f32[64,4,8,128]{3,2,1,0:T(8,128)S(1)} async-done(((f32[64,4,8,128]{3,2,1,0:T(8,128)}), f32[64,4,8,128]{3,2,1,0:T(8,128)S(1)}, u32[]{:S(2)}, u32[]{:S(2)}) %all-to-all-start.1) | async-done | bytes 1048608 | tf_op jit(solution)/shard_map/all_to_all | solution.py:606
  95.8 1.6 %shard_map.113 = f32[8,256,128]{2,1,0:T(8,128)} custom-call(f32[2048,128]{1,0:T(8,128)S(1)} %bitcast.14, f32[8,256,128]{2,1,0:T(8,128)S(1)} %shard_map.112.local_ref, bf16[256,512]{1,0:T(8,128)(2,1)S(1)} %copy-done), custom_call_target="tpu_custom_call" | custom-call | flops 402653184 | bytes 4718592 | tf_op jit(solution)/shard_map/pallas_call | solution.py:405
  (17 shorter events, 0.1 us)
Async XLA Ops:
  2.9 43.0 %all-to-all-start = ((f32[64,4,8,128]{3,2,1,0:T(8,128)}), f32[64,4,8,128]{3,2,1,0:T(8,128)S(1)}, u32[]{:S(2)}, u32[]{:S(2)}) async-start(f32[64,4,8,128]{3,2,1,0:T(8,128)} %bitcast.1), calls=%async_computation | async-start | bytes 2097152 | tf_op jit(solution)/shard_map/all_to_all | solution.py:585
  17.8 0.7 copy-start.4
  18.9 0.7 copy-start.5
  18.9 0.7 copy-start.6
  45.9 7.6 %copy-start.1 = (bf16[2,256,256]{2,1,0:T(8,128)(2,1)S(1)}, bf16[2,256,256]{2,1,0:T(8,128)(2,1)}, u32[]{:S(2)}) copy-start(bf16[2,256,256]{2,1,0:T(8,128)(2,1)} %constant.150.clone.inner_ref) | copy-start | bytes 786436
  45.9 7.6 %copy-start.2 = (bf16[256,512]{1,0:T(8,128)(2,1)S(1)}, bf16[256,512]{1,0:T(8,128)(2,1)}, u32[]{:S(2)}) copy-start(bf16[256,512]{1,0:T(8,128)(2,1)} %constant.148.clone.inverse_ref) | copy-start | bytes 786436
  45.9 7.6 %copy-start.3 = (bf16[256,512]{1,0:T(8,128)(2,1)S(1)}, bf16[256,512]{1,0:T(8,128)(2,1)}, u32[]{:S(2)}) copy-start(bf16[256,512]{1,0:T(8,128)(2,1)} %constant.147.clone.forward_ref) | copy-start | bytes 786436
  46.3 12.3 %collective-permute-start = (f32[320,128]{1,0:T(8,128)S(1)}, f32[320,128]{1,0:T(8,128)S(1)}, u32[]{:S(2)}, u32[]{:S(2)}) collective-permute-start(f32[320,128]{1,0:T(8,128)S(1)} %get-tuple-element.7), channel_id=1, source_target_pairs={{64,128},{128,64},{192,256},{256,192},{320,384},{384,320},{448,0},... | collective-permute-start | bytes 491528 | tf_op jit(solution)/shard_map/ppermute | solution.py:602
  51.4 6.1 %collective-permute-start.1 = (f32[320,128]{1,0:T(8,128)S(1)}, f32[320,128]{1,0:T(8,128)S(1)}, u32[]{:S(2)}, u32[]{:S(2)}) collective-permute-start(f32[320,128]{1,0:T(8,128)S(1)} %get-tuple-element.8), channel_id=1, source_target_pairs={{0,64},{64,0},{128,192},{192,128},{256,320},{320,256},{384,448},{4... | collective-permute-start | bytes 491528 | tf_op jit(solution)/shard_map/ppermute | solution.py:601
  59.8 36.0 %all-to-all-start.1 = ((f32[64,4,8,128]{3,2,1,0:T(8,128)}), f32[64,4,8,128]{3,2,1,0:T(8,128)S(1)}, u32[]{:S(2)}, u32[]{:S(2)}) async-start(f32[64,4,8,128]{3,2,1,0:T(8,128)} %edge_second.1), calls=%async_computation.1 | async-start | bytes 2097152 | tf_op jit(solution)/shard_map/all_to_all | solution.py:606
  67.7 28.2 %copy-start = (bf16[256,512]{1,0:T(8,128)(2,1)S(1)}, bf16[256,512]{1,0:T(8,128)(2,1)}, u32[]{:S(2)}) copy-start(bf16[256,512]{1,0:T(8,128)(2,1)} %constant.146.clone.table_ref) | copy-start | bytes 786436

commit v5 on v4

--- a/solution.py
+++ b/solution.py
@@ -116,10 +116,10 @@
 
 
 def wide_dot(table, high, low):
-    return (
-        dot(table[:, :POINTS], high)
-        + dot(table[:, :POINTS], low)
-        + dot(table[:, POINTS : 2 * POINTS], high)
+    first, second = table[:, :POINTS], table[:, POINTS : 2 * POINTS]
+    return dot(
+        jnp.concatenate([first, first, second], axis=1),
+        jnp.concatenate([high, low, high], axis=0),
     )
 
 
@@ -291,21 +291,24 @@
     owners = out_ref.shape[0] // 2
     result = wide_dot(inverse_ref[...], y_ref[0:POINTS, :], y_ref[POINTS:, :])
     moved = [
-        sum(
-            dot(
-                jnp.concatenate(
-                    [
-                        x_ref[
-                            half + side * HALF : half + (side + 1) * HALF,
-                            q * width : (q + 1) * width,
-                        ]
-                        for q in range(4)
-                    ],
-                    axis=0,
-                ),
-                inner_ref[side],
-            )
-            for half in (0, POINTS)
+        dot(
+            jnp.concatenate(
+                [
+                    jnp.concatenate(
+                        [
+                            x_ref[
+                                half + side * HALF : half + (side + 1) * HALF,
+                                q * width : (q + 1) * width,
+                            ]
+                            for half in (0, POINTS)
+                        ],
+                        axis=1,
+                    )
+                    for q in range(4)
+                ],
+                axis=0,
+            ),
+            jnp.concatenate([inner_ref[side]] * 2, axis=0),
         )
         for side in range(2)
     ]

time: 97.9 us -> 97.9 us (level)
  no operation moved by 1% of the time
where the time goes in v5:
time: 97.9 us; the launch traced here: 97.5 us
  waiting for transfers between devices  52.8 us (54%)
  starting transfers between devices  29.7 us (30%)
  Pallas kernels  11.8 us (12%)
  local copies, waits for them, and re-layouts  1.44 us (1%)
  matrix products  1.12 us (1%)
    all_to_all x1, waiting for transfers between devices, local(): lax.all_to_all(back, group, split_axis=0, concat_axis=0, tiled=True)  25.8 us
    all_to_all x1, waiting for transfers between devices, local(): lax.all_to_all(sent, group, split_axis=0, concat_axis=0, tiled=True)  25.2 us
    all_to_all x1, starting transfers between devices, local(): lax.all_to_all(sent, group, split_axis=0, concat_axis=0, tiled=True)  14.8 us
    pallas_call x5, Pallas kernels, call(): pl.pallas_call(kernel, grid=grid, out_shape=shapes[0] if single else shap...  9.43 us
    all_to_all x1, starting transfers between devices, local(): lax.all_to_all(back, group, split_axis=0, concat_axis=0, tiled=True)  7.83 us
    ppermute x1, starting transfers between devices, local(): second = lax.ppermute(second, 'y', swaps[1])  5.09 us
    pallas_call x2, Pallas kernels, stage_edge(): pl.pallas_call(functools.partial(edge_kernel, odd_band), out_shape=pltpu....  2.34 us
  transfers between devices with their start and end apart: 4, of which 3 were waited for; matrix products, arithmetic and copies ran while one was open for 2% of the time, Pallas kernels for 6%

profile of v5, /device:TPU:1, one launch (start us, length us, event | category | flops | bytes accessed | tf_op | source)
XLA Modules:
  0.0 97.5 jit_solution(477743072459658648)
XLA Ops:
  0.0 2.9 %shard_map.109 = f32[2048,128]{1,0:T(8,128)} custom-call(f32[8,256,128]{2,1,0:T(8,128)} %u_ref.1, bf16[256,512]{1,0:T(8,128)(2,1)} %constant.145.clone.table_hbm), custom_call_target="tpu_custom_call" | custom-call | flops 402653184 | bytes 2621440 | tf_op jit(solution)/shard_map/pallas_call | solution.py:408
  2.9 14.8 %all-to-all-start = ((f32[64,4,8,128]{3,2,1,0:T(8,128)}), f32[64,4,8,128]{3,2,1,0:T(8,128)S(1)}, u32[]{:S(2)}, u32[]{:S(2)}) async-start(f32[64,4,8,128]{3,2,1,0:T(8,128)} %bitcast.1), calls=%async_computation | async-start | bytes 2097152 | tf_op jit(solution)/shard_map/all_to_all | solution.py:588
  17.8 0.7 copy-done.4
  18.5 0.1 fusion.68
  18.6 0.1 fusion.53
  18.8 0.1 broadcast_multiply_fusion.3
  18.8 0.1 broadcast_multiply_fusion.1
  18.9 0.7 copy-done.5
  19.6 0.0 copy-done.6
  19.6 1.1 %fusion.symbol_ref = f32[2,4,128,256]{3,2,1,0:T(8,128)S(1)} fusion(f32[2,1,128,16]{2,3,1,0:T(8,128)S(1)} %get-tuple-element.14, f32[2,1,128,16]{2,3,1,0:T(8,128)S(1)} %get-tuple-element.13, f32[2,1,128,16]{2,3,1,0:T(8,128)S(1)} %get-tuple-element.10, f32[2,1,128,16]{2,3,1,0:T(8,128)S(1)} %get-tuple-element.9, f32[16]{0:T(128)S(1)} %copy-done.5, ...), kind=kOutput, calls=%fused_computation | convolution fusion | flops 50511872 | bytes 1116416 | tf_op jit(solution)/shard_map/dot_general | solution.py:459
  20.7 25.2 %all-to-all-done.r_ref = f32[64,4,8,128]{3,2,1,0:T(8,128)S(1)} async-done(((f32[64,4,8,128]{3,2,1,0:T(8,128)}), f32[64,4,8,128]{3,2,1,0:T(8,128)S(1)}, u32[]{:S(2)}, u32[]{:S(2)}) %all-to-all-start) | async-done | bytes 1048608 | tf_op jit(solution)/shard_map/all_to_all | solution.py:588
  45.9 0.4 shard_map.111
  46.3 5.1 %collective-permute-start = (f32[320,128]{1,0:T(8,128)S(1)}, f32[320,128]{1,0:T(8,128)S(1)}, u32[]{:S(2)}, u32[]{:S(2)}) collective-permute-start(f32[320,128]{1,0:T(8,128)S(1)} %get-tuple-element.7), channel_id=1, source_target_pairs={{64,128},{128,64},{192,256},{256,192},{320,384},{384,320},{448,0},... | collective-permute-start | bytes 491528 | tf_op jit(solution)/shard_map/ppermute | solution.py:605
  51.4 1.9 %collective-permute-start.1 = (f32[320,128]{1,0:T(8,128)S(1)}, f32[320,128]{1,0:T(8,128)S(1)}, u32[]{:S(2)}, u32[]{:S(2)}) collective-permute-start(f32[320,128]{1,0:T(8,128)S(1)} %get-tuple-element.8), channel_id=1, source_target_pairs={{0,64},{64,0},{128,192},{192,128},{256,320},{320,256},{384,448},{4... | collective-permute-start | bytes 491528 | tf_op jit(solution)/shard_map/ppermute | solution.py:604
  53.3 0.1 fusion.65
  53.4 0.1 mul.283.damp_ref
  53.5 2.1 %shard_map.110.partial_ref = f32[64,4,8,128]{3,2,1,0:T(8,128)S(1)} custom-call(f32[4]{0:T(128)S(1)} %mul.283.damp_ref, f32[64,4,8,128]{3,2,1,0:T(8,128)S(1)} %all-to-all-done.r_ref, bf16[256,512]{1,0:T(8,128)(2,1)S(1)} %copy-done.3, f32[2,4,128,256]{3,2,1,0:T(8,128)S(1)} %fusion.symbol_ref, bf16[256,512]{1,0:T(8,128)(2,1)S(1)} %copy-done.2, ...), custom_call_target="tpu_custom_call" | custom-call | flops 1342177280 | bytes 5767200 | tf_op jit(solution)/shard_map/pallas_call | solution.py:408
  55.6 1.8 %collective-permute-done.1.halo_ref = f32[320,128]{1,0:T(8,128)S(1)} collective-permute-done((f32[320,128]{1,0:T(8,128)S(1)}, f32[320,128]{1,0:T(8,128)S(1)}, u32[]{:S(2)}, u32[]{:S(2)}) %collective-permute-start.1) | collective-permute-done | bytes 163872 | tf_op jit(solution)/shard_map/ppermute | solution.py:604
  57.5 1.2 %edge_first.1.refs_0_ = f32[64,4,8,128]{3,2,1,0:T(8,128)} custom-call(s32[1]{0:T(128)} %bitcast.odd_ref, f32[64,4,8,128]{3,2,1,0:T(8,128)S(1)} %shard_map.110.partial_ref, f32[320,128]{1,0:T(8,128)S(1)} %collective-permute-done.1.halo_ref), custom_call_target="tpu_custom_call" | custom-call | flops 5242880 | bytes 1048576 | tf_op jit(solution)/shard_map/edge_first/pallas_call | solution.py:542
  58.6 1.2 %edge_second.1 = f32[64,4,8,128]{3,2,1,0:T(8,128)} custom-call(s32[1]{0:T(128)} %bitcast.odd_ref, f32[64,4,8,128]{3,2,1,0:T(8,128)S(1)} %shard_map.110.partial_ref, f32[320,128]{1,0:T(8,128)S(1)} %collective-permute-done.halo_ref, f32[64,4,8,128]{3,2,1,0:T(8,128)} %edge_first.1.refs_0_), custom_call_target="tpu_custom_call", output_to_operand_aliasing={{}: (3, {})} | custom-call | flops 5242880 | bytes 1048576 | tf_op jit(solution)/shard_map/edge_second/pallas_call | solution.py:542
  59.8 7.8 %all-to-all-start.1 = ((f32[64,4,8,128]{3,2,1,0:T(8,128)}), f32[64,4,8,128]{3,2,1,0:T(8,128)S(1)}, u32[]{:S(2)}, u32[]{:S(2)}) async-start(f32[64,4,8,128]{3,2,1,0:T(8,128)} %edge_second.1), calls=%async_computation.1 | async-start | bytes 2097152 | tf_op jit(solution)/shard_map/all_to_all | solution.py:609
  67.6 2.4 %shard_map.112.local_ref = f32[8,256,128]{2,1,0:T(8,128)S(1)} custom-call(f32[8,256,128]{2,1,0:T(8,128)} %u_ref.1, bf16[256,512]{1,0:T(8,128)(2,1)} %constant.149.clone.friction_ref, bf16[2,256,128]{2,1,0:T(8,128)(2,1)} %constant.151.clone.shift_ref), custom_call_target="tpu_custom_call" | custom-call | flops 402653184 | bytes 2883584 | tf_op jit(solution)/shard_map/pallas_call | solution.py:408
  70.0 25.8 %all-to-all-done.1 = f32[64,4,8,128]{3,2,1,0:T(8,128)S(1)} async-done(((f32[64,4,8,128]{3,2,1,0:T(8,128)}), f32[64,4,8,128]{3,2,1,0:T(8,128)S(1)}, u32[]{:S(2)}, u32[]{:S(2)}) %all-to-all-start.1) | async-done | bytes 1048608 | tf_op jit(solution)/shard_map/all_to_all | solution.py:609
  95.8 1.7 %shard_map.113 = f32[8,256,128]{2,1,0:T(8,128)} custom-call(f32[2048,128]{1,0:T(8,128)S(1)} %bitcast.14, f32[8,256,128]{2,1,0:T(8,128)S(1)} %shard_map.112.local_ref, bf16[256,512]{1,0:T(8,128)(2,1)S(1)} %copy-done), custom_call_target="tpu_custom_call" | custom-call | flops 402653184 | bytes 4718592 | tf_op jit(solution)/shard_map/pallas_call | solution.py:408
  (17 shorter events, 0.1 us)
Async XLA Ops:
  2.9 43.0 %all-to-all-start = ((f32[64,4,8,128]{3,2,1,0:T(8,128)}), f32[64,4,8,128]{3,2,1,0:T(8,128)S(1)}, u32[]{:S(2)}, u32[]{:S(2)}) async-start(f32[64,4,8,128]{3,2,1,0:T(8,128)} %bitcast.1), calls=%async_computation | async-start | bytes 2097152 | tf_op jit(solution)/shard_map/all_to_all | solution.py:588
  17.8 0.7 copy-start.4
  18.9 0.7 copy-start.5
  18.9 0.7 copy-start.6
  45.9 7.6 %copy-start.1 = (bf16[2,256,256]{2,1,0:T(8,128)(2,1)S(1)}, bf16[2,256,256]{2,1,0:T(8,128)(2,1)}, u32[]{:S(2)}) copy-start(bf16[2,256,256]{2,1,0:T(8,128)(2,1)} %constant.150.clone.inner_ref) | copy-start | bytes 786436
  45.9 7.6 %copy-start.2 = (bf16[256,512]{1,0:T(8,128)(2,1)S(1)}, bf16[256,512]{1,0:T(8,128)(2,1)}, u32[]{:S(2)}) copy-start(bf16[256,512]{1,0:T(8,128)(2,1)} %constant.148.clone.inverse_ref) | copy-start | bytes 786436
  45.9 7.6 %copy-start.3 = (bf16[256,512]{1,0:T(8,128)(2,1)S(1)}, bf16[256,512]{1,0:T(8,128)(2,1)}, u32[]{:S(2)}) copy-start(bf16[256,512]{1,0:T(8,128)(2,1)} %constant.147.clone.forward_ref) | copy-start | bytes 786436
  46.3 12.3 %collective-permute-start = (f32[320,128]{1,0:T(8,128)S(1)}, f32[320,128]{1,0:T(8,128)S(1)}, u32[]{:S(2)}, u32[]{:S(2)}) collective-permute-start(f32[320,128]{1,0:T(8,128)S(1)} %get-tuple-element.7), channel_id=1, source_target_pairs={{64,128},{128,64},{192,256},{256,192},{320,384},{384,320},{448,0},... | collective-permute-start | bytes 491528 | tf_op jit(solution)/shard_map/ppermute | solution.py:605
  51.4 6.1 %collective-permute-start.1 = (f32[320,128]{1,0:T(8,128)S(1)}, f32[320,128]{1,0:T(8,128)S(1)}, u32[]{:S(2)}, u32[]{:S(2)}) collective-permute-start(f32[320,128]{1,0:T(8,128)S(1)} %get-tuple-element.8), channel_id=1, source_target_pairs={{0,64},{64,0},{128,192},{192,128},{256,320},{320,256},{384,448},{4... | collective-permute-start | bytes 491528 | tf_op jit(solution)/shard_map/ppermute | solution.py:604
  59.8 36.0 %all-to-all-start.1 = ((f32[64,4,8,128]{3,2,1,0:T(8,128)}), f32[64,4,8,128]{3,2,1,0:T(8,128)S(1)}, u32[]{:S(2)}, u32[]{:S(2)}) async-start(f32[64,4,8,128]{3,2,1,0:T(8,128)} %edge_second.1), calls=%async_computation.1 | async-start | bytes 2097152 | tf_op jit(solution)/shard_map/all_to_all | solution.py:609
  67.6 28.2 %copy-start = (bf16[256,512]{1,0:T(8,128)(2,1)S(1)}, bf16[256,512]{1,0:T(8,128)(2,1)}, u32[]{:S(2)}) copy-start(bf16[256,512]{1,0:T(8,128)(2,1)} %constant.146.clone.table_ref) | copy-start | bytes 786436

commit v6 on v5

--- a/solution.py
+++ b/solution.py
@@ -334,14 +334,23 @@
     return jnp.where((lane >= first_row * NY) & (lane < last_row * NY), weight, 0.0)
 
 
-def edge_kernel(odd_band, odd_ref, partial_ref, halo_ref, *refs):
-    out_ref = refs[-1]
+def edge_kernel(odd_band, odd_ref, partial_ref, halo_ref, out_ref):
     for odd in range(2):
 
         @pl.when(odd_ref[0] == odd)
         def _(band=odd_band if odd else 1 - odd_band):
             for side in range(2):
                 edge_part(band, side, partial_ref, halo_ref, out_ref)
+
+
+def edge_second_kernel(odd_ref, partial_ref, halo_ref, done_ref, out_ref):
+    @pl.when(pl.program_id(0) == 0)
+    def _():
+        out_ref[...] = done_ref[...]
+
+    @pl.when(pl.program_id(0) == 1)
+    def _():
+        edge_kernel(1, odd_ref, partial_ref, halo_ref, out_ref)
 
 
 def edge_part(band, side, partial_ref, halo_ref, out_ref):
@@ -532,29 +541,38 @@
     )
 
 
-def stage_edge(odd, partial, halo, odd_band, back=None):
+def stage_edge_first(odd, partial, halo):
     members, _, planes, cells = partial.shape
-
-    def place(_, odd_ref):
-        return (jnp.where(odd_ref[0] == 1, odd_band, 1 - odd_band), 0, 0, 0)
-
-    given = [] if back is None else [off_chip(back)]
+    return call(
+        functools.partial(edge_kernel, 0),
+        [((members // 2, 4, planes, cells), F32)],
+        (odd, partial, halo),
+        flops=20 * partial.size,
+        smem=1,
+    )
+
+
+def stage_edge_second(odd, partial, halo, done):
+    members, _, planes, cells = partial.shape
+
+    def place(i, odd_ref):
+        return (jnp.where(odd_ref[0] == 1, i, 1 - i), 0, 0, 0)
+
     return pl.pallas_call(
-        functools.partial(edge_kernel, odd_band),
-        out_shape=pltpu.HBM(partial.shape, F32),
+        edge_second_kernel,
+        out_shape=jax.ShapeDtypeStruct(partial.shape, F32),
         grid_spec=pltpu.PrefetchScalarGridSpec(
             num_scalar_prefetch=1,
-            grid=(1,),
-            in_specs=[VMEM_SPEC] * 2 + [pl.BlockSpec(memory_space=pl.ANY)] * len(given),
+            grid=(2,),
+            in_specs=[VMEM_SPEC] * 3,
             out_specs=pl.BlockSpec((members // 2, 4, planes, cells), place),
         ),
-        input_output_aliases={3: 0} if given else {},
         cost_estimate=pl.CostEstimate(
             flops=20 * partial.size, bytes_accessed=4 * partial.size, transcendentals=0
         ),
         compiler_params=pltpu.CompilerParams(vmem_limit_bytes=24 << 20),
-        name="edge_second" if given else "edge_first",
-    )(odd, on_chip(partial), on_chip(halo), *given)
+        name="edge_second",
+    )(odd, on_chip(partial), on_chip(halo), on_chip(done))
 
 
 def stage_backward(panels, here, table):
@@ -604,8 +622,8 @@
     first = lax.ppermute(first, "y", swaps[0])
     second = lax.ppermute(second, "y", swaps[1])
     partial = stage_middle(damp, columns, symbol, table)
-    back = stage_edge(odd, partial, first, 0)
-    back = stage_edge(odd, partial, second, 1, back)
+    done = stage_edge_first(odd, partial, first)
+    back = stage_edge_second(odd, partial, second, done)
     panels = lax.all_to_all(back, group, split_axis=0, concat_axis=0, tiled=True)
     return stage_backward(panels, here, table)
 

time: 97.9 us -> 97.3 us (level)
    pallas_call x2 -> x1, Pallas kernels: 2.34 us -> 1.28 us  [stage_edge_second(): pl.pallas_call(edge_second_kernel, out_shape=jax.ShapeDtypeStruct(partial...]
    pallas_call x5 -> x6, Pallas kernels: 9.43 us -> 9.82 us  [call(): pl.pallas_call(kernel, grid=grid, out_shape=shapes[0] if single else shap...]
  transfers between devices with their start and end apart: 4 -> 4, of which waited for: 3 -> 3; matrix products, arithmetic and copies ran while one was open for 2% -> 2% of each run, Pallas kernels for 6% -> 5%
where the time goes in v6:
time: 97.3 us; the launch traced here: 96.8 us
  waiting for transfers between devices  52.8 us (54%)
  starting transfers between devices  29.7 us (31%)
  Pallas kernels  11.1 us (11%)
  local copies, waits for them, and re-layouts  1.44 us (1%)
  matrix products  1.12 us (1%)
    all_to_all x1, waiting for transfers between devices, local(): lax.all_to_all(back, group, split_axis=0, concat_axis=0, tiled=True)  25.8 us
    all_to_all x1, waiting for transfers between devices, local(): lax.all_to_all(sent, group, split_axis=0, concat_axis=0, tiled=True)  25.2 us
    all_to_all x1, starting transfers between devices, local(): lax.all_to_all(sent, group, split_axis=0, concat_axis=0, tiled=True)  14.8 us
    pallas_call x6, Pallas kernels, call(): pl.pallas_call(kernel, grid=grid, out_shape=shapes[0] if single else shap...  9.82 us
    all_to_all x1, starting transfers between devices, local(): lax.all_to_all(back, group, split_axis=0, concat_axis=0, tiled=True)  7.83 us
    ppermute x1, starting transfers between devices, local(): second = lax.ppermute(second, 'y', swaps[1])  5.09 us
  transfers between devices with their start and end apart: 4, of which 3 were waited for; matrix products, arithmetic and copies ran while one was open for 2% of the time, Pallas kernels for 5%

profile of v6, /device:TPU:1, one launch (start us, length us, event | category | flops | bytes accessed | tf_op | source)
XLA Modules:
  0.0 96.8 jit_solution(11757853380804257380)
XLA Ops:
  0.0 2.9 %shard_map.109 = f32[2048,128]{1,0:T(8,128)} custom-call(f32[8,256,128]{2,1,0:T(8,128)} %u_ref.1, bf16[256,512]{1,0:T(8,128)(2,1)} %constant.145.clone.table_hbm), custom_call_target="tpu_custom_call" | custom-call | flops 402653184 | bytes 2621440 | tf_op jit(solution)/shard_map/pallas_call | solution.py:417
  2.9 14.8 %all-to-all-start = ((f32[64,4,8,128]{3,2,1,0:T(8,128)}), f32[64,4,8,128]{3,2,1,0:T(8,128)S(1)}, u32[]{:S(2)}, u32[]{:S(2)}) async-start(f32[64,4,8,128]{3,2,1,0:T(8,128)} %bitcast.1), calls=%async_computation | async-start | bytes 2097152 | tf_op jit(solution)/shard_map/all_to_all | solution.py:606
  17.8 0.7 copy-done.4
  18.5 0.1 fusion.68
  18.6 0.1 fusion.53
  18.8 0.1 broadcast_multiply_fusion.3
  18.8 0.1 broadcast_multiply_fusion.1
  18.9 0.7 copy-done.5
  19.6 0.0 copy-done.6
  19.6 1.1 %fusion.symbol_ref = f32[2,4,128,256]{3,2,1,0:T(8,128)S(1)} fusion(f32[2,1,128,16]{2,3,1,0:T(8,128)S(1)} %get-tuple-element.14, f32[2,1,128,16]{2,3,1,0:T(8,128)S(1)} %get-tuple-element.13, f32[2,1,128,16]{2,3,1,0:T(8,128)S(1)} %get-tuple-element.10, f32[2,1,128,16]{2,3,1,0:T(8,128)S(1)} %get-tuple-element.9, f32[16]{0:T(128)S(1)} %copy-done.5, ...), kind=kOutput, calls=%fused_computation | convolution fusion | flops 50511872 | bytes 1116416 | tf_op jit(solution)/shard_map/dot_general | solution.py:468
  20.7 25.2 %all-to-all-done.r_ref = f32[64,4,8,128]{3,2,1,0:T(8,128)S(1)} async-done(((f32[64,4,8,128]{3,2,1,0:T(8,128)}), f32[64,4,8,128]{3,2,1,0:T(8,128)S(1)}, u32[]{:S(2)}, u32[]{:S(2)}) %all-to-all-start) | async-done | bytes 1048608 | tf_op jit(solution)/shard_map/all_to_all | solution.py:606
  45.9 0.4 shard_map.111
  46.3 5.1 %collective-permute-start = (f32[320,128]{1,0:T(8,128)S(1)}, f32[320,128]{1,0:T(8,128)S(1)}, u32[]{:S(2)}, u32[]{:S(2)}) collective-permute-start(f32[320,128]{1,0:T(8,128)S(1)} %get-tuple-element.7), channel_id=1, source_target_pairs={{64,128},{128,64},{192,256},{256,192},{320,384},{384,320},{448,0},... | collective-permute-start | bytes 491528 | tf_op jit(solution)/shard_map/ppermute | solution.py:623
  51.4 1.9 %collective-permute-start.1 = (f32[320,128]{1,0:T(8,128)S(1)}, f32[320,128]{1,0:T(8,128)S(1)}, u32[]{:S(2)}, u32[]{:S(2)}) collective-permute-start(f32[320,128]{1,0:T(8,128)S(1)} %get-tuple-element.8), channel_id=1, source_target_pairs={{0,64},{64,0},{128,192},{192,128},{256,320},{320,256},{384,448},{4... | collective-permute-start | bytes 491528 | tf_op jit(solution)/shard_map/ppermute | solution.py:622
  53.3 0.1 fusion.65
  53.4 0.1 mul.283.damp_ref
  53.5 2.1 %shard_map.110.partial_ref = f32[64,4,8,128]{3,2,1,0:T(8,128)S(1)} custom-call(f32[4]{0:T(128)S(1)} %mul.283.damp_ref, f32[64,4,8,128]{3,2,1,0:T(8,128)S(1)} %all-to-all-done.r_ref, bf16[256,512]{1,0:T(8,128)(2,1)S(1)} %copy-done.1, f32[2,4,128,256]{3,2,1,0:T(8,128)S(1)} %fusion.symbol_ref, bf16[256,512]{1,0:T(8,128)(2,1)S(1)} %copy-done.2, ...), custom_call_target="tpu_custom_call" | custom-call | flops 1342177280 | bytes 5767200 | tf_op jit(solution)/shard_map/pallas_call | solution.py:417
  55.6 1.8 %collective-permute-done.1.halo_ref = f32[320,128]{1,0:T(8,128)S(1)} collective-permute-done((f32[320,128]{1,0:T(8,128)S(1)}, f32[320,128]{1,0:T(8,128)S(1)}, u32[]{:S(2)}, u32[]{:S(2)}) %collective-permute-start.1) | collective-permute-done | bytes 163872 | tf_op jit(solution)/shard_map/ppermute | solution.py:622
  57.5 0.4 shard_map.112.done_ref
  57.9 1.3 %edge_second.1 = f32[64,4,8,128]{3,2,1,0:T(8,128)} custom-call(s32[1]{0:T(128)} %bitcast.odd_ref, f32[64,4,8,128]{3,2,1,0:T(8,128)S(1)} %shard_map.110.partial_ref, f32[320,128]{1,0:T(8,128)S(1)} %collective-permute-done.halo_ref, f32[32,4,8,128]{3,2,1,0:T(8,128)S(1)} %shard_map.112.done_ref), custom_call_target="tpu_custom_call" | custom-call | flops 5242880 | bytes 1048576 | tf_op jit(solution)/shard_map/edge_second/pallas_call | solution.py:561
  59.1 7.8 %all-to-all-start.1 = ((f32[64,4,8,128]{3,2,1,0:T(8,128)}), f32[64,4,8,128]{3,2,1,0:T(8,128)S(1)}, u32[]{:S(2)}, u32[]{:S(2)}) async-start(f32[64,4,8,128]{3,2,1,0:T(8,128)} %edge_second.1), calls=%async_computation.1 | async-start | bytes 2097152 | tf_op jit(solution)/shard_map/all_to_all | solution.py:627
  67.0 2.4 %shard_map.113.local_ref = f32[8,256,128]{2,1,0:T(8,128)S(1)} custom-call(f32[8,256,128]{2,1,0:T(8,128)} %u_ref.1, bf16[256,512]{1,0:T(8,128)(2,1)} %constant.149.clone.friction_ref, bf16[2,256,128]{2,1,0:T(8,128)(2,1)} %constant.151.clone.shift_ref), custom_call_target="tpu_custom_call" | custom-call | flops 402653184 | bytes 2883584 | tf_op jit(solution)/shard_map/pallas_call | solution.py:417
  69.4 25.8 %all-to-all-done.1 = f32[64,4,8,128]{3,2,1,0:T(8,128)S(1)} async-done(((f32[64,4,8,128]{3,2,1,0:T(8,128)}), f32[64,4,8,128]{3,2,1,0:T(8,128)S(1)}, u32[]{:S(2)}, u32[]{:S(2)}) %all-to-all-start.1) | async-done | bytes 1048608 | tf_op jit(solution)/shard_map/all_to_all | solution.py:627
  95.1 1.7 %shard_map.114 = f32[8,256,128]{2,1,0:T(8,128)} custom-call(f32[2048,128]{1,0:T(8,128)S(1)} %bitcast.14, f32[8,256,128]{2,1,0:T(8,128)S(1)} %shard_map.113.local_ref, bf16[256,512]{1,0:T(8,128)(2,1)S(1)} %copy-done), custom_call_target="tpu_custom_call" | custom-call | flops 402653184 | bytes 4718592 | tf_op jit(solution)/shard_map/pallas_call | solution.py:417
  (17 shorter events, 0.1 us)
Async XLA Ops:
  2.9 43.0 %all-to-all-start = ((f32[64,4,8,128]{3,2,1,0:T(8,128)}), f32[64,4,8,128]{3,2,1,0:T(8,128)S(1)}, u32[]{:S(2)}, u32[]{:S(2)}) async-start(f32[64,4,8,128]{3,2,1,0:T(8,128)} %bitcast.1), calls=%async_computation | async-start | bytes 2097152 | tf_op jit(solution)/shard_map/all_to_all | solution.py:606
  17.8 0.7 copy-start.4
  18.9 0.7 copy-start.5
  18.9 0.7 copy-start.6
  45.9 7.6 %copy-start.1 = (bf16[256,512]{1,0:T(8,128)(2,1)S(1)}, bf16[256,512]{1,0:T(8,128)(2,1)}, u32[]{:S(2)}) copy-start(bf16[256,512]{1,0:T(8,128)(2,1)} %constant.147.clone.forward_ref) | copy-start | bytes 786436
  45.9 7.6 %copy-start.2 = (bf16[256,512]{1,0:T(8,128)(2,1)S(1)}, bf16[256,512]{1,0:T(8,128)(2,1)}, u32[]{:S(2)}) copy-start(bf16[256,512]{1,0:T(8,128)(2,1)} %constant.148.clone.inverse_ref) | copy-start | bytes 786436
  45.9 7.6 %copy-start.3 = (bf16[2,256,256]{2,1,0:T(8,128)(2,1)S(1)}, bf16[2,256,256]{2,1,0:T(8,128)(2,1)}, u32[]{:S(2)}) copy-start(bf16[2,256,256]{2,1,0:T(8,128)(2,1)} %constant.150.clone.inner_ref) | copy-start | bytes 786436
  46.3 11.6 %collective-permute-start = (f32[320,128]{1,0:T(8,128)S(1)}, f32[320,128]{1,0:T(8,128)S(1)}, u32[]{:S(2)}, u32[]{:S(2)}) collective-permute-start(f32[320,128]{1,0:T(8,128)S(1)} %get-tuple-element.7), channel_id=1, source_target_pairs={{64,128},{128,64},{192,256},{256,192},{320,384},{384,320},{448,0},... | collective-permute-start | bytes 491528 | tf_op jit(solution)/shard_map/ppermute | solution.py:623
  51.4 6.1 %collective-permute-start.1 = (f32[320,128]{1,0:T(8,128)S(1)}, f32[320,128]{1,0:T(8,128)S(1)}, u32[]{:S(2)}, u32[]{:S(2)}) collective-permute-start(f32[320,128]{1,0:T(8,128)S(1)} %get-tuple-element.8), channel_id=1, source_target_pairs={{0,64},{64,0},{128,192},{192,128},{256,320},{320,256},{384,448},{4... | collective-permute-start | bytes 491528 | tf_op jit(solution)/shard_map/ppermute | solution.py:622
  59.1 36.0 %all-to-all-start.1 = ((f32[64,4,8,128]{3,2,1,0:T(8,128)}), f32[64,4,8,128]{3,2,1,0:T(8,128)S(1)}, u32[]{:S(2)}, u32[]{:S(2)}) async-start(f32[64,4,8,128]{3,2,1,0:T(8,128)} %edge_second.1), calls=%async_computation.1 | async-start | bytes 2097152 | tf_op jit(solution)/shard_map/all_to_all | solution.py:627
  67.0 28.2 %copy-start = (bf16[256,512]{1,0:T(8,128)(2,1)S(1)}, bf16[256,512]{1,0:T(8,128)(2,1)}, u32[]{:S(2)}) copy-start(bf16[256,512]{1,0:T(8,128)(2,1)} %constant.146.clone.table_ref) | copy-start | bytes 786436

commit v7 on v5

--- a/solution.py
+++ b/solution.py
@@ -20,7 +20,6 @@
 F32 = jnp.float32
 BF16 = jnp.bfloat16
 HIGHEST_PRECISION = lax.Precision.HIGHEST
-FORWARD_STEPS = 1
 BACKWARD_STEPS = 1
 LOCAL_STEPS = 2
 
@@ -128,31 +127,13 @@
     return (2 * index - (POINTS - 1)).astype(F32) * (1.0 / (60 * POINTS))
 
 
-def forward_kernel(u_hbm, table_hbm, out_ref, u_ref, table_ref, sems):
+def forward_kernel(u_ref, table_ref, out_ref):
     planes, _, cells = u_ref.shape
-    step = planes // FORWARD_STEPS
-    table_copy = pltpu.make_async_copy(table_hbm, table_ref, sems.at[FORWARD_STEPS])
-    copies = [
-        pltpu.make_async_copy(
-            u_hbm.at[pl.ds(i * step, step)], u_ref.at[pl.ds(i * step, step)], sems.at[i]
-        )
-        for i in range(FORWARD_STEPS)
-    ]
-    copies[0].start()
-    table_copy.start()
-    for copy in copies[1:]:
-        copy.start()
-    for i, copy in enumerate(copies):
-        copy.wait()
-        if i == 0:
-            table_copy.wait()
-        parts = [split(u_ref[k]) for k in range(i * step, (i + 1) * step)]
-        high, low = (jnp.concatenate(values, axis=1) for values in zip(*parts))
-        result = wide_dot(table_ref[...], high, low)
-        for k in range(step):
-            out_ref[pl.ds(i * step + k, POINTS, stride=planes), :] = result[
-                :, k * cells : (k + 1) * cells
-            ]
+    parts = [split(u_ref[k]) for k in range(planes)]
+    high, low = (jnp.concatenate(values, axis=1) for values in zip(*parts))
+    result = wide_dot(table_ref[...], high, low)
+    for k in range(planes):
+        out_ref[pl.ds(k, POINTS, stride=planes), :] = result[:, k * cells : (k + 1) * cells]
 
 
 def backward_kernel(w_ref, local_ref, table_ref, out_ref):
@@ -475,14 +456,9 @@
         forward_kernel,
         [((points * planes, cells), F32)],
         (off_chip(density), off_chip(table["forward_second"])),
-        (
-            pltpu.VMEM(density.shape, F32),
-            pltpu.VMEM((points, 2 * points), BF16),
-            pltpu.SemaphoreType.DMA((FORWARD_STEPS + 1,)),
-        ),
         flops=6 * points * points * planes * cells,
         keep=False,
-        in_specs=[pl.BlockSpec(memory_space=pl.ANY)] * 2,
+        in_specs=[VMEM_SPEC] * 2,
     )
     return sent.reshape(points // 4, 4, planes, cells)
 

time: 97.9 us -> 97.9 us (level)
  no operation moved by 1% of the time
where the time goes in v7:
time: 97.9 us; the launch traced here: 97.4 us
  waiting for transfers between devices  52.8 us (54%)
  starting transfers between devices  29.7 us (30%)
  Pallas kernels  11.7 us (12%)
  local copies, waits for them, and re-layouts  1.44 us (1%)
  matrix products  1.12 us (1%)
    all_to_all x1, waiting for transfers between devices, local(): lax.all_to_all(back, group, split_axis=0, concat_axis=0, tiled=True)  25.8 us
    all_to_all x1, waiting for transfers between devices, local(): lax.all_to_all(sent, group, split_axis=0, concat_axis=0, tiled=True)  25.2 us
    all_to_all x1, starting transfers between devices, local(): lax.all_to_all(sent, group, split_axis=0, concat_axis=0, tiled=True)  14.8 us
    pallas_call x5, Pallas kernels, call(): pl.pallas_call(kernel, grid=grid, out_shape=shapes[0] if single else shap...  9.37 us
    all_to_all x1, starting transfers between devices, local(): lax.all_to_all(back, group, split_axis=0, concat_axis=0, tiled=True)  7.83 us
    ppermute x1, starting transfers between devices, local(): second = lax.ppermute(second, 'y', swaps[1])  5.1 us
    pallas_call x2, Pallas kernels, stage_edge(): pl.pallas_call(functools.partial(edge_kernel, odd_band), out_shape=pltpu....  2.34 us
  transfers between devices with their start and end apart: 4, of which 3 were waited for; matrix products, arithmetic and copies ran while one was open for 2% of the time, Pallas kernels for 6%

profile of v7, /device:TPU:1, one launch (start us, length us, event | category | flops | bytes accessed | tf_op | source)
XLA Modules:
  0.0 97.4 jit_solution(2853014327048238654)
XLA Ops:
  0.0 2.8 %shard_map.109 = f32[2048,128]{1,0:T(8,128)} custom-call(f32[8,256,128]{2,1,0:T(8,128)} %u_ref.3, bf16[256,512]{1,0:T(8,128)(2,1)} %constant.145.clone.table_ref), custom_call_target="tpu_custom_call" | custom-call | flops 402653184 | bytes 2621440 | tf_op jit(solution)/shard_map/pallas_call | solution.py:389
  2.8 14.8 %all-to-all-start = ((f32[64,4,8,128]{3,2,1,0:T(8,128)}), f32[64,4,8,128]{3,2,1,0:T(8,128)S(1)}, u32[]{:S(2)}, u32[]{:S(2)}) async-start(f32[64,4,8,128]{3,2,1,0:T(8,128)} %bitcast.1), calls=%async_computation | async-start | bytes 2097152 | tf_op jit(solution)/shard_map/all_to_all | solution.py:564
  17.7 0.7 copy-done.4
  18.4 0.1 fusion.68
  18.5 0.1 fusion.53
  18.7 0.1 broadcast_multiply_fusion.3
  18.8 0.1 broadcast_multiply_fusion.1
  18.8 0.7 copy-done.5
  19.5 0.0 copy-done.6
  19.5 1.1 %fusion.symbol_ref = f32[2,4,128,256]{3,2,1,0:T(8,128)S(1)} fusion(f32[2,1,128,16]{2,3,1,0:T(8,128)S(1)} %get-tuple-element.14, f32[2,1,128,16]{2,3,1,0:T(8,128)S(1)} %get-tuple-element.13, f32[2,1,128,16]{2,3,1,0:T(8,128)S(1)} %get-tuple-element.10, f32[2,1,128,16]{2,3,1,0:T(8,128)S(1)} %get-tuple-element.9, f32[16]{0:T(128)S(1)} %copy-done.5, ...), kind=kOutput, calls=%fused_computation | convolution fusion | flops 50511872 | bytes 1116416 | tf_op jit(solution)/shard_map/dot_general | solution.py:440
  20.6 25.2 %all-to-all-done.r_ref = f32[64,4,8,128]{3,2,1,0:T(8,128)S(1)} async-done(((f32[64,4,8,128]{3,2,1,0:T(8,128)}), f32[64,4,8,128]{3,2,1,0:T(8,128)S(1)}, u32[]{:S(2)}, u32[]{:S(2)}) %all-to-all-start) | async-done | bytes 1048608 | tf_op jit(solution)/shard_map/all_to_all | solution.py:564
  45.8 0.4 shard_map.111
  46.2 5.1 %collective-permute-start = (f32[320,128]{1,0:T(8,128)S(1)}, f32[320,128]{1,0:T(8,128)S(1)}, u32[]{:S(2)}, u32[]{:S(2)}) collective-permute-start(f32[320,128]{1,0:T(8,128)S(1)} %get-tuple-element.7), channel_id=1, source_target_pairs={{64,128},{128,64},{192,256},{256,192},{320,384},{384,320},{448,0},... | collective-permute-start | bytes 491528 | tf_op jit(solution)/shard_map/ppermute | solution.py:581
  51.3 1.9 %collective-permute-start.1 = (f32[320,128]{1,0:T(8,128)S(1)}, f32[320,128]{1,0:T(8,128)S(1)}, u32[]{:S(2)}, u32[]{:S(2)}) collective-permute-start(f32[320,128]{1,0:T(8,128)S(1)} %get-tuple-element.8), channel_id=1, source_target_pairs={{0,64},{64,0},{128,192},{192,128},{256,320},{320,256},{384,448},{4... | collective-permute-start | bytes 491528 | tf_op jit(solution)/shard_map/ppermute | solution.py:580
  53.3 0.1 fusion.65
  53.3 0.1 mul.283.damp_ref
  53.4 2.1 %shard_map.110.partial_ref = f32[64,4,8,128]{3,2,1,0:T(8,128)S(1)} custom-call(f32[4]{0:T(128)S(1)} %mul.283.damp_ref, f32[64,4,8,128]{3,2,1,0:T(8,128)S(1)} %all-to-all-done.r_ref, bf16[256,512]{1,0:T(8,128)(2,1)S(1)} %copy-done.3, f32[2,4,128,256]{3,2,1,0:T(8,128)S(1)} %fusion.symbol_ref, bf16[256,512]{1,0:T(8,128)(2,1)S(1)} %copy-done.2, ...), custom_call_target="tpu_custom_call" | custom-call | flops 1342177280 | bytes 5767200 | tf_op jit(solution)/shard_map/pallas_call | solution.py:389
  55.6 1.8 %collective-permute-done.1.halo_ref = f32[320,128]{1,0:T(8,128)S(1)} collective-permute-done((f32[320,128]{1,0:T(8,128)S(1)}, f32[320,128]{1,0:T(8,128)S(1)}, u32[]{:S(2)}, u32[]{:S(2)}) %collective-permute-start.1) | collective-permute-done | bytes 163872 | tf_op jit(solution)/shard_map/ppermute | solution.py:580
  57.4 1.2 %edge_first.1.refs_0_ = f32[64,4,8,128]{3,2,1,0:T(8,128)} custom-call(s32[1]{0:T(128)} %bitcast.odd_ref, f32[64,4,8,128]{3,2,1,0:T(8,128)S(1)} %shard_map.110.partial_ref, f32[320,128]{1,0:T(8,128)S(1)} %collective-permute-done.1.halo_ref), custom_call_target="tpu_custom_call" | custom-call | flops 5242880 | bytes 1048576 | tf_op jit(solution)/shard_map/edge_first/pallas_call | solution.py:518
  58.6 1.2 %edge_second.1 = f32[64,4,8,128]{3,2,1,0:T(8,128)} custom-call(s32[1]{0:T(128)} %bitcast.odd_ref, f32[64,4,8,128]{3,2,1,0:T(8,128)S(1)} %shard_map.110.partial_ref, f32[320,128]{1,0:T(8,128)S(1)} %collective-permute-done.halo_ref, f32[64,4,8,128]{3,2,1,0:T(8,128)} %edge_first.1.refs_0_), custom_call_target="tpu_custom_call", output_to_operand_aliasing={{}: (3, {})} | custom-call | flops 5242880 | bytes 1048576 | tf_op jit(solution)/shard_map/edge_second/pallas_call | solution.py:518
  59.7 7.8 %all-to-all-start.1 = ((f32[64,4,8,128]{3,2,1,0:T(8,128)}), f32[64,4,8,128]{3,2,1,0:T(8,128)S(1)}, u32[]{:S(2)}, u32[]{:S(2)}) async-start(f32[64,4,8,128]{3,2,1,0:T(8,128)} %edge_second.1), calls=%async_computation.1 | async-start | bytes 2097152 | tf_op jit(solution)/shard_map/all_to_all | solution.py:585
  67.6 2.4 %shard_map.112.local_ref = f32[8,256,128]{2,1,0:T(8,128)S(1)} custom-call(f32[8,256,128]{2,1,0:T(8,128)} %u_ref.3, bf16[256,512]{1,0:T(8,128)(2,1)} %constant.149.clone.friction_ref, bf16[2,256,128]{2,1,0:T(8,128)(2,1)} %constant.151.clone.shift_ref), custom_call_target="tpu_custom_call" | custom-call | flops 402653184 | bytes 2883584 | tf_op jit(solution)/shard_map/pallas_call | solution.py:389
  69.9 25.8 %all-to-all-done.1 = f32[64,4,8,128]{3,2,1,0:T(8,128)S(1)} async-done(((f32[64,4,8,128]{3,2,1,0:T(8,128)}), f32[64,4,8,128]{3,2,1,0:T(8,128)S(1)}, u32[]{:S(2)}, u32[]{:S(2)}) %all-to-all-start.1) | async-done | bytes 1048608 | tf_op jit(solution)/shard_map/all_to_all | solution.py:585
  95.7 1.7 %shard_map.113 = f32[8,256,128]{2,1,0:T(8,128)} custom-call(f32[2048,128]{1,0:T(8,128)S(1)} %bitcast.14, f32[8,256,128]{2,1,0:T(8,128)S(1)} %shard_map.112.local_ref, bf16[256,512]{1,0:T(8,128)(2,1)S(1)} %copy-done), custom_call_target="tpu_custom_call" | custom-call | flops 402653184 | bytes 4718592 | tf_op jit(solution)/shard_map/pallas_call | solution.py:389
  (17 shorter events, 0.1 us)
Async XLA Ops:
  2.8 43.0 %all-to-all-start = ((f32[64,4,8,128]{3,2,1,0:T(8,128)}), f32[64,4,8,128]{3,2,1,0:T(8,128)S(1)}, u32[]{:S(2)}, u32[]{:S(2)}) async-start(f32[64,4,8,128]{3,2,1,0:T(8,128)} %bitcast.1), calls=%async_computation | async-start | bytes 2097152 | tf_op jit(solution)/shard_map/all_to_all | solution.py:564
  17.7 0.7 copy-start.4
  18.8 0.7 copy-start.5
  18.8 0.7 copy-start.6
  45.8 7.6 %copy-start.1 = (bf16[2,256,256]{2,1,0:T(8,128)(2,1)S(1)}, bf16[2,256,256]{2,1,0:T(8,128)(2,1)}, u32[]{:S(2)}) copy-start(bf16[2,256,256]{2,1,0:T(8,128)(2,1)} %constant.150.clone.inner_ref) | copy-start | bytes 786436
  45.8 7.6 %copy-start.2 = (bf16[256,512]{1,0:T(8,128)(2,1)S(1)}, bf16[256,512]{1,0:T(8,128)(2,1)}, u32[]{:S(2)}) copy-start(bf16[256,512]{1,0:T(8,128)(2,1)} %constant.148.clone.inverse_ref) | copy-start | bytes 786436
  45.8 7.6 %copy-start.3 = (bf16[256,512]{1,0:T(8,128)(2,1)S(1)}, bf16[256,512]{1,0:T(8,128)(2,1)}, u32[]{:S(2)}) copy-start(bf16[256,512]{1,0:T(8,128)(2,1)} %constant.147.clone.forward_ref) | copy-start | bytes 786436
  46.2 12.3 %collective-permute-start = (f32[320,128]{1,0:T(8,128)S(1)}, f32[320,128]{1,0:T(8,128)S(1)}, u32[]{:S(2)}, u32[]{:S(2)}) collective-permute-start(f32[320,128]{1,0:T(8,128)S(1)} %get-tuple-element.7), channel_id=1, source_target_pairs={{64,128},{128,64},{192,256},{256,192},{320,384},{384,320},{448,0},... | collective-permute-start | bytes 491528 | tf_op jit(solution)/shard_map/ppermute | solution.py:581
  51.3 6.1 %collective-permute-start.1 = (f32[320,128]{1,0:T(8,128)S(1)}, f32[320,128]{1,0:T(8,128)S(1)}, u32[]{:S(2)}, u32[]{:S(2)}) collective-permute-start(f32[320,128]{1,0:T(8,128)S(1)} %get-tuple-element.8), channel_id=1, source_target_pairs={{0,64},{64,0},{128,192},{192,128},{256,320},{320,256},{384,448},{4... | collective-permute-start | bytes 491528 | tf_op jit(solution)/shard_map/ppermute | solution.py:580
  59.7 36.0 %all-to-all-start.1 = ((f32[64,4,8,128]{3,2,1,0:T(8,128)}), f32[64,4,8,128]{3,2,1,0:T(8,128)S(1)}, u32[]{:S(2)}, u32[]{:S(2)}) async-start(f32[64,4,8,128]{3,2,1,0:T(8,128)} %edge_second.1), calls=%async_computation.1 | async-start | bytes 2097152 | tf_op jit(solution)/shard_map/all_to_all | solution.py:585
  67.6 28.2 %copy-start = (bf16[256,512]{1,0:T(8,128)(2,1)S(1)}, bf16[256,512]{1,0:T(8,128)(2,1)}, u32[]{:S(2)}) copy-start(bf16[256,512]{1,0:T(8,128)(2,1)} %constant.146.clone.table_ref) | copy-start | bytes 786436
